TPU v7x, 32 devices: a whole 2x2x4 slice. The times are simulated.
32 devices in a mesh: tok: 4 (over z), hid: 8 (over y, x, core).
Axes of the slice: x: 2, y: 2, z: 4, core: 2. Of those that a mesh axis runs over, the one named last changes fastest.
Arguments:
- tokens: bfloat16 [2048, 1024], P('tok', 'hid'), may hold values from -6 to 6
- cotangent: bfloat16 [2048, 1024], P('tok', 'hid'), may hold values from -6 to 6
- frozen_in: bfloat16 [1024, 16384], P('tok', 'hid'), may hold values from -0.1875 to 0.1875
- frozen_out: bfloat16 [16384, 1024], P('hid', 'tok'), may hold values from -0.046875 to 0.046875
- input_adapter_first: bfloat16 [1024, 128], P('hid'), may hold values from -0.1875 to 0.1875
- input_adapter_second: bfloat16 [128, 16384], P(None, 'hid'), may hold values from -0.5 to 0.5
- adapter_out_a: bfloat16 [16384, 128], P('hid'), may hold values from -0.046875 to 0.046875
- adapter_out_b: bfloat16 [128, 1024], replicated, may hold values from -0.5 to 0.5
Outputs:
- input_gradient: float32 [2048, 1024], P('tok', 'hid')
- grad_in_a: float32 [1024, 128], P('hid')
- grad_in_b: float32 [128, 16384], P(None, 'hid')
- grad_out_a: float32 [16384, 128], P('hid')
- grad_out_b: float32 [128, 1024], P(None, 'hid')
All inputs are finite; a program needn't handle non-finite values.
Results may differ from a plain program's by a relative error of at most 0.0029.
Values may be sent and summed in bfloat16 or wider, within the bound.
A program may use at most 64 MiB of HBM per device.

v0:
```python
import math

import jax
import jax.numpy as jnp
from jax import lax
from jax.sharding import PartitionSpec as P

ADAPTER_SCALE = 0.5
GELU_K = 0.7978845608
GELU_C = 0.044715


def gelu_pair(pre_activation):
    tangent = jnp.tanh(
        GELU_K * (pre_activation + GELU_C * pre_activation * pre_activation * pre_activation)
    )
    value_out = 0.5 * pre_activation * (1.0 + tangent)
    slopes = 0.5 * (1.0 + tangent) + 0.5 * pre_activation * (1.0 - tangent * tangent) * GELU_K * (
        1.0 + 3.0 * GELU_C * pre_activation * pre_activation
    )
    return (value_out, slopes)


def local(
    tokens,
    cotangent,
    frozen_in,
    frozen_out,
    input_adapter_first,
    input_adapter_second,
    adapter_out_a,
    adapter_out_b,
):
    highest_precision = lax.Precision.HIGHEST
    device_local_rows = tokens.shape[0]
    rank_width = input_adapter_second.shape[0]
    gradient_scale = ADAPTER_SCALE / math.sqrt(device_local_rows * lax.axis_size("tok"))
    full_tokens, full_cotan = (
        lax.all_gather(tokens, "hid", axis=1, tiled=True),
        lax.all_gather(cotangent, "hid", axis=1, tiled=True),
    )
    in_rows = lax.all_gather(frozen_in, "tok", axis=0, tiled=True)
    in_a_full = lax.all_gather(input_adapter_first, "hid", axis=0, tiled=True)
    lowrank_input = jnp.dot(full_tokens, in_a_full, preferred_element_type=jnp.float32)
    second_float = input_adapter_second.astype(jnp.float32)
    out_a_float = adapter_out_a.astype(jnp.float32)
    pre_activation = jnp.dot(
        full_tokens, in_rows, preferred_element_type=jnp.float32
    ) + ADAPTER_SCALE * jnp.dot(lowrank_input, second_float, precision=highest_precision)
    value_out, slopes = gelu_pair(pre_activation)
    hidden_act = value_out.astype(jnp.bfloat16)
    backward_lowrank = jnp.einsum(
        "td,rd->tr", full_cotan, adapter_out_b, preferred_element_type=jnp.float32
    )
    rank_out = jnp.dot(hidden_act, adapter_out_a, preferred_element_type=jnp.float32)
    dense_backward = jnp.einsum(
        "td,fd->tf",
        full_cotan,
        lax.all_gather(frozen_out, "tok", axis=1, tiled=True),
        preferred_element_type=jnp.float32,
    )
    dense_backward = dense_backward + ADAPTER_SCALE * jnp.dot(
        backward_lowrank, out_a_float.T, precision=highest_precision
    )
    grad_pre = (dense_backward * slopes).astype(jnp.bfloat16)
    rank_backward = jnp.einsum(
        "tf,rf->tr", grad_pre, input_adapter_second, preferred_element_type=jnp.float32
    )
    dense_in = jnp.einsum("tf,df->td", grad_pre, in_rows, preferred_element_type=jnp.float32)
    grad_out_a = gradient_scale * jnp.dot(
        hidden_act.astype(jnp.float32).T, backward_lowrank, precision=highest_precision
    )
    grad_in_b = gradient_scale * jnp.dot(
        lowrank_input.T, grad_pre.astype(jnp.float32), precision=highest_precision
    )
    in_a_float = in_a_full.astype(jnp.float32)
    dx_term = dense_in + ADAPTER_SCALE * jnp.dot(
        rank_backward, in_a_float.T, precision=highest_precision
    )
    out_term = jnp.dot(rank_out.T, full_cotan.astype(jnp.float32), precision=highest_precision)
    in_term = jnp.dot(rank_backward.T, full_tokens.astype(jnp.float32), precision=highest_precision)
    rank_terms = jnp.concatenate([out_term, in_term], axis=0)
    input_gradient, rank_local = (
        lax.psum_scatter(dx_term, "hid", scatter_dimension=1, tiled=True),
        lax.psum_scatter(rank_terms, "hid", scatter_dimension=1, tiled=True),
    )
    grad_out_a, grad_in_b, rank_total = lax.psum((grad_out_a, grad_in_b, rank_local), "tok")
    grad_out_b = gradient_scale * rank_total[:rank_width]
    grad_in_a = gradient_scale * rank_total[rank_width:].T
    return (input_gradient, grad_in_a, grad_in_b, grad_out_a, grad_out_b)


def solution(mesh):
    in_specs = (
        P("tok", "hid"),
        P("tok", "hid"),
        P("tok", "hid"),
        P("hid", "tok"),
        P("hid", None),
        P(None, "hid"),
        P("hid", None),
        P(),
    )
    out_specs = (P("tok", "hid"), P("hid", None), P(None, "hid"), P("hid", None), P(None, "hid"))
    return jax.shard_map(local, mesh=mesh, in_specs=in_specs, out_specs=out_specs, check_vma=False)
```

profile of v0, /device:TPU:0, one launch (start us, length us, event | category | flops | bytes accessed | tf_op | source)
XLA Modules:
  0.0 421.3 jit_solution(1950593718763780741)
XLA Ops:
  7.2 0.0 copy-start
  7.2 0.0 all-gather.5.cloned.1.call-start
  7.2 0.7 all-gather.5.cloned.1.call-update
  7.9 0.0 all-gather.9.cloned.1.call-start
  8.0 0.7 all-gather.9.cloned.1.call-update
  8.7 0.0 all-gather.11.cloned.1.call-start
  8.7 0.7 all-gather.11.cloned.1.call-update
  9.4 0.0 all-gather.7.cloned.1.call-start
  9.4 0.5 all-gather.7.cloned.1.call-update
  10.0 0.0 reduce-scatter.5.cloned.1.call-start
  10.0 11.0 %all_gather.19 = bf16[1024,128]{1,0:T(8,128)(2,1)S(1)} all-gather(bf16[128,128]{1,0:T(8,128)(2,1)} %param.12), channel_id=1, replica_groups=mesh['tok'=4,'hid'=8] {'hid'}, dimensions={0}, use_global_device_ids=true | all-gather | bytes 294912 | tf_op jit(solution)/shard_map/all_gather | solution.py:43
  21.0 15.1 %all-gather.5.cloned.1.call-done = bf16[512,1024]{1,0:T(8,128)(2,1)} async-done(((bf16[512,128]{1,0:T(8,128)(2,1)}), bf16[512,1024]{1,0:T(8,128)(2,1)}) %all-gather.5.cloned.1.call-update) | async-done | bytes 1048592 | tf_op jit(solution)/shard_map/all_gather | solution.py:40
  36.1 1.7 fusion.9
  37.8 23.7 %all-gather.9.cloned.1.call-done = bf16[512,1024]{1,0:T(8,128)(2,1)} async-done(((bf16[512,128]{1,0:T(8,128)(2,1)}), bf16[512,1024]{1,0:T(8,128)(2,1)}) %all-gather.9.cloned.1.call-update) | async-done | bytes 1048592 | tf_op jit(solution)/shard_map/all_gather | solution.py:39
  61.5 1.7 fusion.11
  63.1 0.0 copy-start.6
  63.2 80.7 %all-gather.11.cloned.1.call-done = bf16[1024,2048]{1,0:T(8,128)(2,1)} async-done(((bf16[256,2048]{1,0:T(8,128)(2,1)}), bf16[1024,2048]{1,0:T(8,128)(2,1)}) %all-gather.11.cloned.1.call-update) | async-done | bytes 4194320 | tf_op jit(solution)/shard_map/all_gather | solution.py:42
  143.8 4.8 %fusion.10 = f32[512,2048]{1,0:T(8,128)S(1)} fusion(bf16[512,1024]{1,0:T(8,128)(2,1)} %all-gather.9.cloned.1.call-done, bf16[1024,2048]{1,0:T(8,128)(2,1)} %all-gather.11.cloned.1.call-done), kind=kOutput, calls=%fused_computation.20 | convolution fusion | flops 2147483648 | bytes 9437184 | tf_op jit(solution)/shard_map/dot_general | solution.py:47
  148.7 0.0 copy-done.6
  148.7 0.0 copy-done
  148.7 0.0 copy-start.3
  148.7 5.9 %multiply_convert_fusion = (bf16[512,2048]{1,0:T(8,128)(2,1)}, f32[512,2048]{1,0:T(8,128)}) fusion(f32[512,2048]{1,0:T(8,128)S(1)} %fusion.10, f32[512,128]{1,0:T(8,128)S(1)} %fusion.11, bf16[128,2048]{1,0:T(8,128)(2,1)S(1)} %copy-done), kind=kOutput, calls=%fused_computation.9 | convolution fusion | flops 1622147072 | bytes 11272192 | tf_op jit(solution)/shard_map/dot_general | solution.py:49
  154.6 69.7 %all-gather.7.cloned.1.call-done = bf16[2048,1024]{1,0:T(8,128)(2,1)} async-done(((bf16[2048,256]{1,0:T(8,128)(2,1)}), bf16[2048,1024]{1,0:T(8,128)(2,1)}) %all-gather.7.cloned.1.call-update) | async-done | bytes 4194320 | tf_op jit(solution)/shard_map/all_gather | solution.py:59
  224.3 0.0 copy-done.3
  224.3 0.0 copy-start.7
  224.3 0.0 copy-start.8
  224.3 4.7 %fusion.8 = f32[512,2048]{1,0:T(8,128)S(1)} fusion(bf16[512,1024]{1,0:T(8,128)(2,1)S(1)} %copy-done.3, bf16[2048,1024]{1,0:T(8,128)(2,1)} %all-gather.7.cloned.1.call-done), kind=kOutput, calls=%fused_computation.18 | convolution fusion | flops 2147483648 | bytes 9437184 | tf_op jit(solution)/shard_map/td,fd->tf/dot_general | solution.py:56
  229.0 0.0 copy-done.7
  229.0 0.0 copy-done.8
  229.0 0.0 copy-start.1
  229.1 5.1 %fusion.6 = bf16[512,2048]{1,0:T(8,128)(2,1)S(1)} fusion(f32[512,2048]{1,0:T(8,128)S(1)} %copy-done.8, f32[512,2048]{1,0:T(8,128)S(1)} %fusion.8, f32[512,128]{1,0:T(8,128)S(1)} %fusion.9, bf16[2048,128]{1,0:T(8,128)(2,1)S(1)} %copy-done.7), kind=kOutput, calls=%fused_computation.8 | convolution fusion | flops 1632632832 | bytes 11272192 | tf_op jit(solution)/shard_map/dot_general | solution.py:62
  234.1 0.0 copy-start.5
  234.1 0.0 copy-start.4
  234.1 0.7 fusion.13
  234.8 0.0 copy-done.1
  234.9 0.7 fusion.14
  235.6 0.0 copy-done.5
  235.6 0.7 fusion.16
  236.2 0.0 copy-done.4
  236.3 0.7 fusion.15
  236.9 1.1 pad_maximum_fusion
  238.0 0.0 reduce-scatter.5.cloned.1.call-update
  238.0 0.0 all-reduce.3.cloned.1.call-start
  238.1 0.0 copy-start.2
  238.1 3.1 convolution_multiply_fusion.1
  241.2 0.0 copy-done.2
  241.2 3.3 convolution_multiply_fusion
  244.5 27.9 %reduce-scatter.5.cloned.1.call-done = f32[256,128]{1,0:T(8,128)} async-done(((f32[256,1024]{1,0:T(8,128)}), f32[256,128]{1,0:T(8,128)}) %reduce-scatter.5.cloned.1.call-update) | async-done | bytes 131088 | tf_op jit(solution)/shard_map/reduce_scatter | solution.py:85
  272.4 0.0 all-reduce.3.cloned.1.call-update
  272.4 0.0 reduce-scatter.3.cloned.1.call-start
  272.4 4.5 %fusion.12 = f32[512,1024]{1,0:T(8,128)S(1)} fusion(bf16[512,2048]{1,0:T(8,128)(2,1)S(1)} %fusion.6, bf16[1024,2048]{1,0:T(8,128)(2,1)} %all-gather.11.cloned.1.call-done), kind=kOutput, calls=%fused_computation.22 | convolution fusion | flops 2147483648 | bytes 8388608 | tf_op jit(solution)/shard_map/tf,df->td/dot_general | solution.py:69
  277.0 2.4 multiply_add_fusion.2
  279.4 0.0 reduce-scatter.3.cloned.1.call-update
  279.4 86.5 %all-reduce.3.cloned.1.call-done = (f32[256,128]{1,0:T(8,128)}, f32[128,2048]{1,0:T(8,128)}, f32[2048,128]{1,0:T(8,128)}) async-done(((f32[256,128]{1,0:T(8,128)}, f32[128,2048]{1,0:T(8,128)}, f32[2048,128]{1,0:T(8,128)}), (f32[256,128]{1,0:T(8,128)}, f32[128,2048]{1,0:T(8,128)}, f32[2048,128]{1,0:T(8,128)})) %all-reduce.3.cloned.1.call-update) | async-done | bytes 2228240 | tf_op jit(solution)/shard_map/psum | solution.py:87
  365.8 1.5 slice_multiply_fusion
  367.4 0.7 copy.13
  368.1 41.8 %reduce-scatter.3.cloned.1.call-done = f32[512,128]{1,0:T(8,128)} async-done(((f32[512,1024]{1,0:T(8,128)}), f32[512,128]{1,0:T(8,128)}) %reduce-scatter.3.cloned.1.call-update) | async-done | bytes 262160 | tf_op jit(solution)/shard_map/reduce_scatter | solution.py:84
  409.9 2.3 copy.17
  412.2 2.3 copy.18
Async XLA Ops:
  7.2 141.5 %copy-start = (bf16[128,2048]{1,0:T(8,128)(2,1)S(1)}, bf16[128,2048]{1,0:T(8,128)(2,1)}, u32[]{:S(2)}) copy-start(bf16[128,2048]{1,0:T(8,128)(2,1)} %param.13) | copy-start | bytes 1572868
  7.2 28.9 %all-gather.5.cloned.1.call-start = ((), (), s32[]{:S(2)}) async-start(), calls=%async_computation.2 | async-start | bytes 1179648 | tf_op jit(solution)/shard_map/all_gather | solution.py:40
  7.9 53.6 %all-gather.9.cloned.1.call-start = ((), (), s32[]{:S(2)}) async-start(), calls=%async_computation.4 | async-start | bytes 1179648 | tf_op jit(solution)/shard_map/all_gather | solution.py:39
  8.7 135.2 %all-gather.11.cloned.1.call-start = ((), (), s32[]{:S(2)}) async-start(), calls=%async_computation.5 | async-start | bytes 5242880 | tf_op jit(solution)/shard_map/all_gather | solution.py:42
  9.4 214.9 %all-gather.7.cloned.1.call-start = ((), (), s32[]{:S(2)}) async-start(), calls=%async_computation.3 | async-start | bytes 5242880 | tf_op jit(solution)/shard_map/all_gather | solution.py:59
  10.0 262.4 %reduce-scatter.5.cloned.1.call-start = ((), (), s32[]{:S(2)}) async-start(), calls=%async_computation.7 | async-start | bytes 1179648 | tf_op jit(solution)/shard_map/reduce_scatter | solution.py:85
  63.1 85.5 %copy-start.6 = (f32[512,128]{1,0:T(8,128)}, f32[512,128]{1,0:T(8,128)S(1)}, u32[]{:S(2)}) copy-start(f32[512,128]{1,0:T(8,128)S(1)} %fusion.11) | copy-start | bytes 786436
  148.7 75.6 %copy-start.3 = (bf16[512,1024]{1,0:T(8,128)(2,1)S(1)}, bf16[512,1024]{1,0:T(8,128)(2,1)}, u32[]{:S(2)}) copy-start(bf16[512,1024]{1,0:T(8,128)(2,1)} %all-gather.5.cloned.1.call-done) | copy-start | bytes 3145732
  224.3 4.7 %copy-start.7 = (bf16[2048,128]{1,0:T(8,128)(2,1)S(1)}, bf16[2048,128]{1,0:T(8,128)(2,1)}, u32[]{:S(2)}) copy-start(bf16[2048,128]{1,0:T(8,128)(2,1)} %param.14) | copy-start | bytes 1572868
  224.3 4.7 %copy-start.8 = (f32[512,2048]{1,0:T(8,128)S(1)}, f32[512,2048]{1,0:T(8,128)}, u32[]{:S(2)}) copy-start(f32[512,2048]{1,0:T(8,128)} %get-tuple-element.16) | copy-start | bytes 12582916
  229.0 5.8 %copy-start.1 = (bf16[512,2048]{1,0:T(8,128)(2,1)S(1)}, bf16[512,2048]{1,0:T(8,128)(2,1)}, u32[]{:S(2)}) copy-start(bf16[512,2048]{1,0:T(8,128)(2,1)} %get-tuple-element.15) | copy-start | bytes 6291460
  234.1 1.5 copy-start.5
  234.1 2.1 copy-start.4
  238.0 127.8 %all-reduce.3.cloned.1.call-start = ((), (), s32[]{:S(2)}) async-start(), calls=%async_computation.8 | async-start | bytes 4456448 | tf_op jit(solution)/shard_map/psum | solution.py:87
  238.1 3.1 copy-start.2
  272.4 137.5 %reduce-scatter.3.cloned.1.call-start = ((), (), s32[]{:S(2)}) async-start(), calls=%async_computation.6 | async-start | bytes 2359296 | tf_op jit(solution)/shard_map/reduce_scatter | solution.py:84
Sparse Core Ops, SparseCore 0:
  9.9 26.1 all-gather.4
  38.0 23.4 all-gather.8
  63.1 80.7 all-gather.10
  145.2 79.0 all-gather.6
  238.1 34.1 reduce-scatter.4
  275.4 90.4 all-reduce.2
  369.7 40.1 reduce-scatter.2
where the time goes:
time: 422 us; the launch traced here: 421 us
  waiting for transfers between devices  348 us (82%)
  matrix products  39.9 us (9%)
  between operations  14.3 us (3%)
  blocking collectives  11 us (3%)
  local copies, waits for them, and re-layouts  5.33 us (1%)
    psum x1, waiting for transfers between devices, local(): lax.psum((grad_out_a, grad_in_b, rank_local), 'tok')  86.5 us
    all_gather x1, waiting for transfers between devices, local(): in_rows = lax.all_gather(frozen_in, 'tok', axis=0, tiled=True)  80.7 us
    all_gather x1, waiting for transfers between devices, local(): lax.all_gather(frozen_out, 'tok', axis=1, tiled=True)  69.7 us
    reduce_scatter x1, waiting for transfers between devices, local(): lax.psum_scatter(dx_term, 'hid', scatter_dimension=1, tiled=True)  41.8 us
    reduce_scatter x1, waiting for transfers between devices, local(): lax.psum_scatter(rank_terms, 'hid', scatter_dimension=1, tiled=True)  27.9 us
    all_gather x1, waiting for transfers between devices, local(): lax.all_gather(tokens, 'hid', axis=1, tiled=True)  23.7 us
    all_gather x1, waiting for transfers between devices, local(): lax.all_gather(cotangent, 'hid', axis=1, tiled=True)  15.1 us
    all_gather x1, blocking collectives, local(): in_a_full = lax.all_gather(input_adapter_first, 'hid', axis=0, tiled=True)  11 us
  transfers between devices with their start and end apart: 7, of which 7 were waited for; matrix products, arithmetic and copies ran while one was open for 7% of the time, Pallas kernels for 0%

commit v1 on v0

--- a/solution.py
+++ b/solution.py
@@ -8,6 +8,8 @@
 ADAPTER_SCALE = 0.5
 GELU_K = 0.7978845608
 GELU_C = 0.044715
+F32 = jnp.float32
+BF16 = jnp.bfloat16
 
 
 def gelu_pair(pre_activation):
@@ -21,7 +23,88 @@
     return (value_out, slopes)
 
 
-def local(
+def halves(value):
+    high = lax.reduce_precision(value, exponent_bits=8, mantissa_bits=7)
+    return jnp.concatenate([high.astype(BF16), (value - high).astype(BF16)], axis=1)
+
+
+def dot(left, right, dims):
+    return lax.dot_general(left, right, (dims, ((), ())), preferred_element_type=F32)
+
+
+def gather_inputs(tokens, cotangent, frozen_in, frozen_out, in_a):
+    rows, rank = tokens.shape[0], in_a.shape[1]
+    n_tok = lax.axis_size("tok")
+    both = lax.all_gather(jnp.stack([tokens, cotangent]), "tok", axis=1, tiled=True)
+    both = lax.all_gather(both, "hid", axis=2, tiled=True)
+    in_a_full = lax.all_gather(in_a, "hid", axis=0, tiled=True)
+    w_in = lax.all_to_all(frozen_in, "tok", split_axis=1, concat_axis=0, tiled=True)
+    w_out = lax.all_to_all(frozen_out, "tok", split_axis=0, concat_axis=1, tiled=True)
+    return both[0], both[1], w_in, w_out, in_a_full
+
+
+def reduce_outputs(dense, terms):
+    n_tok, n_hid = lax.axis_size("tok"), lax.axis_size("hid")
+    stacked = jnp.concatenate([dense, terms], axis=0).astype(BF16)
+    split = lax.all_to_all(
+        stacked.reshape(stacked.shape[0], n_hid, -1).transpose(1, 0, 2),
+        "hid", split_axis=0, concat_axis=0, tiled=True,
+    )
+    over_hid = jnp.sum(split.astype(F32), axis=0).astype(BF16)
+    count = dense.shape[0]
+    mine = over_hid[:count].reshape(n_tok, count // n_tok, -1)
+    shared = jnp.broadcast_to(over_hid[count:], (n_tok,) + over_hid[count:].shape)
+    over_tok = lax.all_to_all(
+        jnp.concatenate([mine, shared], axis=1), "tok", split_axis=0, concat_axis=0, tiled=True
+    )
+    total = jnp.sum(over_tok.astype(F32), axis=0)
+    return total[: count // n_tok], total[count // n_tok :]
+
+
+def local(tokens, cotangent, frozen_in, frozen_out, in_a, in_b, out_a, out_b):
+    n_tok, t = lax.axis_size("tok"), lax.axis_index("tok")
+    rank = in_b.shape[0]
+    count = tokens.shape[0] * n_tok
+    scale = ADAPTER_SCALE / math.sqrt(count)
+    width = frozen_in.shape[1] // n_tok
+    x, c, w_in, w_out, in_a_full = gather_inputs(tokens, cotangent, frozen_in, frozen_out, in_a)
+    second = lax.dynamic_slice_in_dim(in_b, t * width, width, 1)
+    first = lax.dynamic_slice_in_dim(out_a, t * width, width, 0)
+    half_second = (ADAPTER_SCALE * second).astype(BF16)
+    half_first = (ADAPTER_SCALE * first).astype(BF16)
+    half_in_a = (ADAPTER_SCALE * in_a_full).astype(BF16)
+    low_in = halves(dot(x, in_a_full, ((1,), (0,))))
+    back_low = halves(dot(c, out_b, ((1,), (1,))))
+    pre = dot(x, w_in, ((1,), (0,))) + dot(
+        low_in, jnp.concatenate([half_second, half_second], axis=0), ((1,), (0,))
+    )
+    value_out, slopes = gelu_pair(pre)
+    act = value_out.astype(BF16)
+    dense_back = dot(c, w_out, ((1,), (1,))) + dot(
+        back_low, jnp.concatenate([half_first, half_first], axis=1), ((1,), (1,))
+    )
+    grad_pre = (dense_back * slopes).astype(BF16)
+    oa = dot(act, back_low, ((0,), (0,)))
+    oa = scale * (oa[:, :rank] + oa[:, rank:])
+    ib = dot(low_in, grad_pre, ((0,), (0,)))
+    ib = scale * (ib[:rank] + ib[rank:])
+    grad_out_a = lax.all_gather(oa.astype(BF16), "tok", axis=0, tiled=True).astype(F32)
+    grad_in_b = lax.all_gather(ib.astype(BF16), "tok", axis=1, tiled=True).astype(F32)
+    rank_out = halves(dot(act, first, ((1,), (0,))))
+    rank_back = halves(dot(grad_pre, second, ((1,), (1,))))
+    dense = dot(grad_pre, w_in, ((1,), (1,))) + dot(
+        rank_back, jnp.concatenate([half_in_a, half_in_a], axis=1), ((1,), (1,))
+    )
+    out_term = dot(rank_out, c, ((0,), (0,)))
+    in_term = dot(rank_back, x, ((0,), (0,)))
+    terms = scale * jnp.concatenate(
+        [out_term[:rank] + out_term[rank:], in_term[:rank] + in_term[rank:]], axis=0
+    )
+    input_gradient, total = reduce_outputs(dense, terms)
+    return (input_gradient, total[rank:].T, grad_in_b, grad_out_a, total[:rank])
+
+
+def local_by_rows(
     tokens,
     cotangent,
     frozen_in,
@@ -102,4 +185,8 @@
         P(),
     )
     out_specs = (P("tok", "hid"), P("hid", None), P(None, "hid"), P("hid", None), P(None, "hid"))
-    return jax.shard_map(local, mesh=mesh, in_specs=in_specs, out_specs=out_specs, check_vma=False)
+    def body(*arrays):
+        share = arrays[2].shape[1] // lax.axis_size("tok")
+        return local(*arrays) if share % 128 == 0 else local_by_rows(*arrays)
+
+    return jax.shard_map(body, mesh=mesh, in_specs=in_specs, out_specs=out_specs, check_vma=False)

time: 422 us -> 268 us (0.64)
  waiting for transfers between devices: 348 us -> 120 us
  blocking collectives: 11 us -> 53.6 us
  starting transfers between devices: 0.27 us -> 16 us
  other arithmetic: 2.6 us -> 13.7 us
    all_gather x4 -> x2, waiting for transfers between devices: 189 us -> 31.8 us  [the longest x1 31.8 us: gather_inputs(): lax.all_gather(jnp.stack([tokens, cotangent]), 'tok', axis=1, tiled=True)]
    all_to_all x0 -> x4, waiting for transfers between devices: none -> 88 us  [the longest x1 53.2 us: reduce_outputs(): lax.all_to_all(stacked.reshape(stacked.shape[0], n_hid, -1).transpose(1,...]
    psum x1 -> x0, waiting for transfers between devices: 86.5 us -> none  [local(): lax.psum((grad_out_a, grad_in_b, rank_local), 'tok')]
    reduce_scatter x2 -> x0, waiting for transfers between devices: 69.6 us -> none  [the longest x1 41.8 us: local(): lax.psum_scatter(dx_term, 'hid', scatter_dimension=1, tiled=True)]
    all_gather x1 -> x3, blocking collectives: 11 us -> 53.6 us  [the longest x1 27.8 us: local(): lax.all_gather(ib.astype(BF16), 'tok', axis=1, tiled=True).astype(F32)]
    all_to_all x0 -> x4, starting transfers between devices: none -> 15.9 us  [the longest x1 4.85 us: reduce_outputs(): lax.all_to_all(stacked.reshape(stacked.shape[0], n_hid, -1).transpose(1,...]
  transfers between devices with their start and end apart: 7 -> 6, of which waited for: 7 -> 4; matrix products, arithmetic and copies ran while one was open for 7% -> 5% of each run, Pallas kernels for 0% -> 0%
where the time goes in v1:
time: 268 us; the launch traced here: 267 us
  waiting for transfers between devices  120 us (45%)
  blocking collectives  53.6 us (20%)
  matrix products  43.3 us (16%)
  starting transfers between devices  16 us (6%)
  between operations  14.5 us (5%)
  other arithmetic  13.7 us (5%)
  local copies, waits for them, and re-layouts  6.09 us (2%)
    all_to_all x1, waiting for transfers between devices, reduce_outputs(): lax.all_to_all(stacked.reshape(stacked.shape[0], n_hid, -1).transpose(1,...  53.2 us
    dot_general x14, matrix products, dot(): lax.dot_general(left, right, (dims, ((), ())), preferred_element_type=F32)  43.3 us
    all_gather x1, waiting for transfers between devices, gather_inputs(): lax.all_gather(jnp.stack([tokens, cotangent]), 'tok', axis=1, tiled=True)  31.8 us
    all_gather x1, blocking collectives, local(): lax.all_gather(ib.astype(BF16), 'tok', axis=1, tiled=True).astype(F32)  27.8 us
    all_to_all x1, waiting for transfers between devices, gather_inputs(): lax.all_to_all(frozen_out, 'tok', split_axis=0, concat_axis=1, tiled=True)  24.2 us
    all_gather x1, blocking collectives, local(): lax.all_gather(oa.astype(BF16), 'tok', axis=0, tiled=True).astype(F32)  15.3 us
    all_to_all x1, waiting for transfers between devices, gather_inputs(): lax.all_to_all(frozen_in, 'tok', split_axis=1, concat_axis=0, tiled=True)  10.7 us
    all_gather x1, blocking collectives, gather_inputs(): in_a_full = lax.all_gather(in_a, 'hid', axis=0, tiled=True)  10.6 us
  transfers between devices with their start and end apart: 6, of which 4 were waited for; matrix products, arithmetic and copies ran while one was open for 5% of the time, Pallas kernels for 0%

profile of v1, /device:TPU:0, one launch (start us, length us, event | category | flops | bytes accessed | tf_op | source)
XLA Modules:
  0.0 267.2 jit_solution(12069626225748256646)
XLA Ops:
  7.2 0.0 copy-start
  7.2 0.0 all-gather.3.cloned.1.call-start
  7.2 1.8 pad_maximum_fusion.10
  9.0 0.0 all-gather.3.cloned.1.call-update
  9.1 0.0 all-gather.5.cloned.1.call-start
  9.1 31.8 %all-gather.3.cloned.1.call-done = bf16[2,2048,128]{2,1,0:T(8,128)(2,1)} async-done(((bf16[2,512,128]{2,1,0:T(8,128)(2,1)}), bf16[2,2048,128]{2,1,0:T(8,128)(2,1)}) %all-gather.3.cloned.1.call-update) | async-done | bytes 1048592 | tf_op jit(solution)/shard_map/all_gather | solution.py:38
  40.9 0.0 all-gather.5.cloned.1.call-update
  40.9 3.5 %all-to-all-start = ((bf16[4,512,256]{2,1,0:T(8,128)(2,1)}), bf16[4,512,256]{2,1,0:T(8,128)(2,1)S(1)}, u32[]{:S(2)}, u32[]{:S(2)}) async-start(bf16[4,512,256]{2,1,0:T(8,128)(2,1)} %bitcast.48), calls=%async_computation | async-start | bytes 2097152 | tf_op jit(solution)/shard_map/all_to_all | solution.py:42
  44.5 0.0 copy-done.5
  44.5 1.3 copy.32
  45.8 24.2 %all-to-all-done = bf16[4,512,256]{2,1,0:T(8,128)(2,1)S(1)} async-done(((bf16[4,512,256]{2,1,0:T(8,128)(2,1)}), bf16[4,512,256]{2,1,0:T(8,128)(2,1)S(1)}, u32[]{:S(2)}, u32[]{:S(2)}) %all-to-all-start) | async-done | bytes 1048608 | tf_op jit(solution)/shard_map/all_to_all | solution.py:42
  69.9 3.5 %all-to-all-start.1 = ((bf16[256,4,512]{0,2,1:T(8,128)(2,1)}), bf16[256,4,512]{0,2,1:T(8,128)(2,1)S(1)}, u32[]{:S(2)}, u32[]{:S(2)}) async-start(bf16[256,4,512]{0,2,1:T(8,128)(2,1)} %bitcast.7), calls=%async_computation.1 | async-start | bytes 2097152 | tf_op jit(solution)/shard_map/all_to_all | solution.py:41
  73.5 10.6 %all_gather.17 = bf16[1024,128]{1,0:T(8,128)(2,1)S(1)} all-gather(bf16[128,128]{1,0:T(8,128)(2,1)S(1)} %copy-done.16), channel_id=1, replica_groups=mesh['tok'=4,'hid'=8] {'hid'}, dimensions={0}, use_global_device_ids=true | all-gather | bytes 294912 | tf_op jit(solution)/shard_map/all_gather | solution.py:40
  84.1 1.0 dynamic-slice_multiply_fusion
  85.1 1.6 dynamic-slice_multiply_fusion.1
  86.7 1.3 copy.31
  88.0 10.7 %all-to-all-done.1 = bf16[256,4,512]{0,2,1:T(8,128)(2,1)S(1)} async-done(((bf16[256,4,512]{0,2,1:T(8,128)(2,1)}), bf16[256,4,512]{0,2,1:T(8,128)(2,1)S(1)}, u32[]{:S(2)}, u32[]{:S(2)}) %all-to-all-start.1) | async-done | bytes 1048608 | tf_op jit(solution)/shard_map/all_to_all | solution.py:41
  98.7 0.5 copy.33
  99.3 0.0 copy-start.6
  99.3 0.0 all-gather.5.cloned.1.call-done
  99.3 4.1 %reduce-precision_convert_fusion.2 = (bf16[2048,128]{0,1:T(8,128)(2,1)S(1)}, bf16[2048,128]{0,1:T(8,128)(2,1)S(1)}) fusion(bf16[1024,128]{1,0:T(8,128)(2,1)} %copy-done.9, bf16[2,2048,1024]{2,1,0:T(8,128)(2,1)} %all-gather.5.cloned.1.call-done), kind=kOutput, calls=%fused_computation.27 | convolution fusion | flops 537919488 | bytes 5505024 | tf_op jit(solution)/shard_map/dot_general | solution.py:32
  103.4 5.0 %fusion.12 = f32[2048,512]{1,0:T(8,128)S(1)} fusion(bf16[1024,512]{1,0:T(8,128)(2,1)S(1)} %bitcast.49, bf16[2,2048,1024]{2,1,0:T(8,128)(2,1)} %all-gather.5.cloned.1.call-done), kind=kOutput, calls=%fused_computation.20 | convolution fusion | flops 2147483648 | bytes 9437184 | tf_op jit(solution)/shard_map/dot_general | solution.py:32
  108.4 0.0 copy-done.6
  108.4 0.0 copy-done.10
  108.4 0.0 copy-done.12
  108.4 0.0 slice-start
  108.5 0.8 convolution_add_fusion
  109.2 0.0 copy-start.2
  109.2 0.0 slice-start.1
  109.2 4.1 %reduce-precision_convert_fusion = (bf16[2048,128]{0,1:T(8,128)(2,1)S(1)}, bf16[2048,128]{0,1:T(8,128)(2,1)S(1)}) fusion(bf16[2048,128]{1,0:T(8,128)(2,1)} %param.14, s32[]{:T(128)S(6)} %select_n.4, f32[2048,512]{1,0:T(8,128)S(1)} %convolution_add_fusion), kind=kOutput, calls=%fused_computation.23 | convolution fusion | flops 278921216 | bytes 5373956 | tf_op jit(solution)/shard_map/dot_general | solution.py:32
  113.4 0.1 slice-done.1
  113.5 1.5 reduce-precision_convert_fusion.3
  115.0 2.3 fusion.9
  117.4 0.0 copy-start.7
  117.4 3.4 %fusion.6 = bf16[2048,512]{1,0:T(8,128)(2,1)S(1)} fusion(f32[2048,512]{1,0:T(8,128)S(1)} %convolution_add_fusion, f32[2048,512]{1,0:T(8,128)S(1)} %fusion.9, bf16[2048,128]{0,1:T(8,128)(2,1)S(1)} %get-tuple-element.35, bf16[2048,128]{0,1:T(8,128)(2,1)S(1)} %get-tuple-element.34, bf16[512,128]{1,0:T(8,128)(2,1)S(1)} %copy-done.15), kind=kOutput, calls=%fused_computation.10 | convolution fusion | flops 560463872 | bytes 11665408 | tf_op jit(solution)/shard_map/dot_general | solution.py:32
  120.9 1.9 reduce-precision_convert_fusion.1
  122.8 5.6 %fusion.50 = f32[2048,1024]{0,1:T(8,128)} fusion(bf16[2048,512]{1,0:T(8,128)(2,1)S(1)} %fusion.6, bf16[1024,512]{1,0:T(8,128)(2,1)S(1)} %bitcast.50), kind=kOutput, calls=%fused_computation.82 | convolution fusion | flops 2147483648 | bytes 11534336 | tf_op jit(solution)/shard_map/dot_general | solution.py:32
  128.4 0.0 copy-done.3
  128.4 1.2 fusion.7
  129.7 0.1 slice_add_fusion.1
  129.7 0.2 copy.40
  129.9 3.4 %fusion.10 = f32[256,1024]{1,0:T(8,128)S(1)} fusion(bf16[2,2048,1024]{2,1,0:T(8,128)(2,1)} %all-gather.5.cloned.1.call-done, bf16[2048,128]{0,1:T(8,128)(2,1)S(1)} %get-tuple-element.33, bf16[2048,128]{0,1:T(8,128)(2,1)S(1)} %get-tuple-element.32), kind=kOutput, calls=%fused_computation.18 | convolution fusion | flops 1075838976 | bytes 6291456 | tf_op jit(solution)/shard_map/dot_general | solution.py:32
  133.4 0.1 slice_add_fusion
  133.4 0.2 copy.41
  133.6 0.1 fusion.20
  133.7 4.6 %add_convert_fusion = bf16[2048,1024]{0,1:T(8,128)(2,1)S(1)} fusion(f32[2048,1024]{0,1:T(8,128)} %fusion.50, bf16[2048,128]{0,1:T(8,128)(2,1)S(1)} %get-tuple-element.33, bf16[2048,128]{0,1:T(8,128)(2,1)S(1)} %get-tuple-element.32, bf16[1024,128]{1,0:T(8,128)(2,1)S(1)} %broadcast_multiply_fusion), kind=kOutput, calls=%fused_computation | convolution fusion | flops 1081081856 | bytes 13893632 | tf_op jit(solution)/shard_map/dot_general | solution.py:32
  138.4 2.6 maximum_bitcast_fusion
  141.0 4.8 %all-to-all-start.2 = ((bf16[8,2304,128]{1,2,0:T(8,128)(2,1)}), bf16[8,2304,128]{1,2,0:T(8,128)(2,1)}, u32[]{:S(2)}, u32[]{:S(2)}) async-start(bf16[8,2304,128]{1,2,0:T(8,128)(2,1)} %maximum_bitcast_fusion), calls=%async_computation.2 | async-start | bytes 9437184 | tf_op jit(solution)/shard_map/all_to_all | solution.py:49
  145.9 0.0 copy-done.4
  145.9 1.5 fusion.21
  147.4 53.2 %all-to-all-done.2 = bf16[8,2304,128]{1,2,0:T(8,128)(2,1)} async-done(((bf16[8,2304,128]{1,2,0:T(8,128)(2,1)}), bf16[8,2304,128]{1,2,0:T(8,128)(2,1)}, u32[]{:S(2)}, u32[]{:S(2)}) %all-to-all-start.2) | async-done | bytes 4718624 | tf_op jit(solution)/shard_map/all_to_all | solution.py:49
  200.6 3.2 %reduce_sum.21 = bf16[2304,128]{0,1:T(8,128)(2,1)S(1)} reduce(bf16[8,2304,128]{1,2,0:T(8,128)(2,1)} %all-to-all-done.2, bf16[]{:T(256)} %constant.10.clone.1), dimensions={0}, to_apply=%region_0.0 | reduce | flops 2064384 | bytes 5308418 | tf_op jit(solution)/shard_map/reduce_sum | solution.py:53
  203.9 0.9 pad_maximum_fusion.3
  204.9 4.0 %all-to-all-start.3 = ((bf16[4,768,128]{1,2,0:T(8,128)(2,1)}), bf16[4,768,128]{1,2,0:T(8,128)(2,1)S(1)}, u32[]{:S(2)}, u32[]{:S(2)}) async-start(bf16[4,768,128]{1,2,0:T(8,128)(2,1)} %pad_maximum_fusion.3), calls=%async_computation.3 | async-start | bytes 1572864 | tf_op jit(solution)/shard_map/all_to_all | solution.py:57
  208.9 27.8 %all_gather.18 = bf16[128,2048]{1,0:T(8,128)(2,1)S(1)} all-gather(bf16[128,512]{1,0:T(8,128)(2,1)S(1)} %fusion.29), channel_id=1, replica_groups=mesh['tok'=4,'hid'=8] {'tok'}, dimensions={1}, use_global_device_ids=true | all-gather | bytes 655360 | tf_op jit(solution)/shard_map/all_gather | solution.py:92
  236.8 1.1 convert_element_type.61
  237.8 3.8 %fusion.22 = f32[512,256]{1,0:T(8,128)S(1)} fusion(bf16[2048,128]{0,1:T(8,128)(2,1)S(1)} %copy-done.20, bf16[2048,128]{0,1:T(8,128)(2,1)S(1)} %copy-done.18, f32[2048,512]{1,0:T(8,128)} %copy-done.2), kind=kOutput, calls=%fused_computation.44 | convolution fusion | flops 548405248 | bytes 5767168 | tf_op jit(solution)/shard_map/dot_general | solution.py:32
  241.7 15.3 %all_gather.19 = bf16[2048,128]{1,0:T(8,128)(2,1)S(1)} all-gather(bf16[512,128]{1,0:T(8,128)(2,1)S(1)} %fusion.27), channel_id=1, replica_groups=mesh['tok'=4,'hid'=8] {'tok'}, dimensions={0}, use_global_device_ids=true | all-gather | bytes 655360 | tf_op jit(solution)/shard_map/all_gather | solution.py:91
  256.9 1.0 convert_element_type.63
  258.0 0.0 all-to-all-done.3
  258.0 0.1 convert_reduce_fusion
  258.1 0.6 fusion.49
  258.7 0.8 copy.38
  259.6 0.7 copy.39
  (42 shorter events, 0.3 us)
Async XLA Ops:
  7.2 106.2 %copy-start = (bf16[128,1024]{1,0:T(8,128)(2,1)S(1)}, bf16[128,1024]{1,0:T(8,128)(2,1)}, u32[]{:S(2)}) copy-start(bf16[128,1024]{1,0:T(8,128)(2,1)} %param.15) | copy-start | bytes 786436
  7.2 37.3 %copy-start.5 = (bf16[256,2048]{1,0:T(8,128)(2,1)S(1)}, bf16[256,2048]{1,0:T(8,128)(2,1)}, u32[]{:S(2)}) copy-start(bf16[256,2048]{1,0:T(8,128)(2,1)} %param.10) | copy-start | bytes 3145732
  7.2 66.3 %copy-start.16 = (bf16[128,128]{1,0:T(8,128)(2,1)S(1)}, bf16[128,128]{1,0:T(8,128)(2,1)}, u32[]{:S(2)}) copy-start(bf16[128,128]{1,0:T(8,128)(2,1)} %param.12) | copy-start | bytes 98308
  7.2 33.7 %all-gather.3.cloned.1.call-start = ((), (), s32[]{:S(2)}) async-start(), calls=%async_computation.4 | async-start | bytes 1310720 | tf_op jit(solution)/shard_map/all_gather | solution.py:38
  9.1 90.2 %all-gather.5.cloned.1.call-start = ((), (), s32[]{:S(2)}) async-start(), calls=%async_computation.5 | async-start | bytes 9437184 | tf_op jit(solution)/shard_map/all_gather | solution.py:39
  40.9 29.0 %all-to-all-start = ((bf16[4,512,256]{2,1,0:T(8,128)(2,1)}), bf16[4,512,256]{2,1,0:T(8,128)(2,1)S(1)}, u32[]{:S(2)}, u32[]{:S(2)}) async-start(bf16[4,512,256]{2,1,0:T(8,128)(2,1)} %bitcast.48), calls=%async_computation | async-start | bytes 2097152 | tf_op jit(solution)/shard_map/all_to_all | solution.py:42
  69.9 28.8 %all-to-all-start.1 = ((bf16[256,4,512]{0,2,1:T(8,128)(2,1)}), bf16[256,4,512]{0,2,1:T(8,128)(2,1)S(1)}, u32[]{:S(2)}, u32[]{:S(2)}) async-start(bf16[256,4,512]{0,2,1:T(8,128)(2,1)} %bitcast.7), calls=%async_computation.1 | async-start | bytes 2097152 | tf_op jit(solution)/shard_map/all_to_all | solution.py:41
  84.1 14.7 %copy-start.9 = (bf16[1024,128]{1,0:T(8,128)(2,1)}, bf16[1024,128]{1,0:T(8,128)(2,1)S(1)}, u32[]{:S(2)}) copy-start(bf16[1024,128]{1,0:T(8,128)(2,1)S(1)} %all_gather.17) | copy-start | bytes 786436
  99.3 9.1 %copy-start.6 = (bf16[4,256,512]{2,1,0:T(8,128)(2,1)}, bf16[4,256,512]{2,1,0:T(8,128)(2,1)S(1)}, u32[]{:S(2)}) copy-start(bf16[4,256,512]{2,1,0:T(8,128)(2,1)S(1)} %copy.33) | copy-start | bytes 3145732
  103.4 5.0 %copy-start.10 = (bf16[2048,128]{0,1:T(8,128)(2,1)}, bf16[2048,128]{0,1:T(8,128)(2,1)S(1)}, u32[]{:S(2)}) copy-start(bf16[2048,128]{0,1:T(8,128)(2,1)S(1)} %get-tuple-element.36) | copy-start | bytes 1572868
  103.4 5.0 %copy-start.12 = (bf16[2048,128]{0,1:T(8,128)(2,1)}, bf16[2048,128]{0,1:T(8,128)(2,1)S(1)}, u32[]{:S(2)}) copy-start(bf16[2048,128]{0,1:T(8,128)(2,1)S(1)} %get-tuple-element.37) | copy-start | bytes 1572868
  108.4 4.9 %slice-start = ((s8[8388608]{0:T(1024)(128)(4,1)}), s8[4194304]{0:T(1024)(128)(4,1)S(1)}, s32[]{:S(2)}) async-start(s8[8388608]{0:T(1024)(128)(4,1)} %bitcast.54), calls=%async_computation.6 | async-start | bytes 8388608
  109.2 8.2 %copy-start.2 = (f32[2048,512]{1,0:T(8,128)}, f32[2048,512]{1,0:T(8,128)S(1)}, u32[]{:S(2)}) copy-start(f32[2048,512]{1,0:T(8,128)S(1)} %convolution_add_fusion) | copy-start | bytes 12582916
  109.2 4.2 %slice-start.1 = ((s8[8388608]{0:T(1024)(128)(4,1)}), s8[4194304]{0:T(1024)(128)(4,1)S(1)}, s32[]{:S(2)}) async-start(s8[8388608]{0:T(1024)(128)(4,1)} %bitcast.54), calls=%async_computation.7 | async-start | bytes 8388608
  113.5 1.5 copy-start.8
  115.0 2.4 copy-start.17
  115.0 2.4 copy-start.19
  115.0 2.4 copy-start.15
  117.4 5.3 %copy-start.7 = (bf16[4,256,512]{2,1,0:T(8,128)(2,1)S(1)}, bf16[4,256,512]{2,1,0:T(8,128)(2,1)}, u32[]{:S(2)}) copy-start(bf16[4,256,512]{2,1,0:T(8,128)(2,1)} %copy-done.6) | copy-start | bytes 3145732
  120.9 7.5 %copy-start.3 = (bf16[2048,512]{1,0:T(8,128)(2,1)}, bf16[2048,512]{1,0:T(8,128)(2,1)S(1)}, u32[]{:S(2)}) copy-start(bf16[2048,512]{1,0:T(8,128)(2,1)S(1)} %fusion.6) | copy-start | bytes 6291460
  141.0 4.9 %copy-start.4 = (bf16[2048,512]{1,0:T(8,128)(2,1)S(1)}, bf16[2048,512]{1,0:T(8,128)(2,1)}, u32[]{:S(2)}) copy-start(bf16[2048,512]{1,0:T(8,128)(2,1)} %copy-done.3) | copy-start | bytes 6291460
  141.0 4.9 %copy-start.11 = (bf16[2048,128]{0,1:T(8,128)(2,1)S(1)}, bf16[2048,128]{0,1:T(8,128)(2,1)}, u32[]{:S(2)}) copy-start(bf16[2048,128]{0,1:T(8,128)(2,1)} %copy-done.10) | copy-start | bytes 1572868
  141.0 4.9 %copy-start.13 = (bf16[2048,128]{0,1:T(8,128)(2,1)S(1)}, bf16[2048,128]{0,1:T(8,128)(2,1)}, u32[]{:S(2)}) copy-start(bf16[2048,128]{0,1:T(8,128)(2,1)} %copy-done.12) | copy-start | bytes 1572868
  141.0 59.6 %all-to-all-start.2 = ((bf16[8,2304,128]{1,2,0:T(8,128)(2,1)}), bf16[8,2304,128]{1,2,0:T(8,128)(2,1)}, u32[]{:S(2)}, u32[]{:S(2)}) async-start(bf16[8,2304,128]{1,2,0:T(8,128)(2,1)} %maximum_bitcast_fusion), calls=%async_computation.2 | async-start | bytes 9437184 | tf_op jit(solution)/shard_map/all_to_all | solution.py:49
  147.4 61.5 %copy-start.14 = (f32[256,512]{1,0:T(8,128)S(1)}, f32[256,512]{1,0:T(8,128)}, u32[]{:S(2)}) copy-start(f32[256,512]{1,0:T(8,128)} %fusion.21) | copy-start | bytes 1572868
  203.8 34.0 %copy-start.18 = (bf16[2048,128]{0,1:T(8,128)(2,1)S(1)}, bf16[2048,128]{0,1:T(8,128)(2,1)}, u32[]{:S(2)}) copy-start(bf16[2048,128]{0,1:T(8,128)(2,1)} %copy-done.17) | copy-start | bytes 1572868
  203.8 34.0 %copy-start.20 = (bf16[2048,128]{0,1:T(8,128)(2,1)S(1)}, bf16[2048,128]{0,1:T(8,128)(2,1)}, u32[]{:S(2)}) copy-start(bf16[2048,128]{0,1:T(8,128)(2,1)} %copy-done.19) | copy-start | bytes 1572868
  204.9 53.1 %all-to-all-start.3 = ((bf16[4,768,128]{1,2,0:T(8,128)(2,1)}), bf16[4,768,128]{1,2,0:T(8,128)(2,1)S(1)}, u32[]{:S(2)}, u32[]{:S(2)}) async-start(bf16[4,768,128]{1,2,0:T(8,128)(2,1)} %pad_maximum_fusion.3), calls=%async_computation.3 | async-start | bytes 1572864 | tf_op jit(solution)/shard_map/all_to_all | solution.py:57
  237.8 22.5 %copy-start.1 = (bf16[128,1024]{1,0:T(8,128)(2,1)S(1)}, bf16[128,1024]{1,0:T(8,128)(2,1)}, u32[]{:S(2)}) copy-start(bf16[128,1024]{1,0:T(8,128)(2,1)} %param.15) | copy-start | bytes 786436
Sparse Core Ops, SparseCore 0:
  10.2 30.6 all-gather.2
  42.8 56.2 all-gather.4

commit v2 on v1

--- a/solution.py
+++ b/solution.py
@@ -1,8 +1,11 @@
+import functools
 import math
 
 import jax
 import jax.numpy as jnp
 from jax import lax
+from jax.experimental import pallas as pl
+from jax.experimental.pallas import tpu as pltpu
 from jax.sharding import PartitionSpec as P
 
 ADAPTER_SCALE = 0.5
@@ -43,22 +46,179 @@
     return both[0], both[1], w_in, w_out, in_a_full
 
 
-def reduce_outputs(dense, terms):
+def reduce_kernel(
+    n_tok, n_hid, dense, terms, oa, ib,
+    dx_out, terms_out, oa_out, ib_out,
+    core_d, core_t, send_d, send_t, recv_d, recv_t, kept_d, kept_t, tok_send, tok_recv,
+    all_t, all_oa, all_ib,
+    core_sem, chip_sem, tok_sem, term_sem, grad_sem,
+):
+    t, h = lax.axis_index("tok"), lax.axis_index("hid")
+    n_chip = n_hid // 2
+    chip, core = h // 2, h % 2
+    rows, cols = dx_out.shape
+    count = terms.shape[0]
+    width = oa.shape[0]
+
+    def remote(source, target, sems, where):
+        return pltpu.make_async_remote_copy(
+            src_ref=source, dst_ref=target, send_sem=sems[0], recv_sem=sems[1],
+            device_id=where, device_id_type=pl.DeviceIdType.MESH,
+        )
+
+    sibling = (t, 2 * chip + 1 - core)
+    chips = [(t, 2 * ((chip + e) % n_chip) + core) for e in range(n_chip)]
+    toks = [((t + d) % n_tok, h) for d in range(n_tok)]
+    barrier = pltpu.get_barrier_semaphore()
+    for where in [sibling] + chips[1:] + toks[1:]:
+        pl.semaphore_signal(barrier, inc=1, device_id=where, device_id_type=pl.DeviceIdType.MESH)
+    pl.semaphore_wait(barrier, n_chip + n_tok - 1)
+
+    def block(index, parity):
+        return pl.ds(pl.multiple_of((2 * index + parity) * cols, cols), cols)
+
+    def tok_rows(d):
+        return pl.ds(pl.multiple_of(((t + d) % n_tok) * rows, rows), rows)
+
+    chunks = [None] + list(range(1, n_tok)) + [0]
+    core_copies, chip_copies, tok_copies = [], [], []
+    for q, d in enumerate(chunks):
+        group = []
+        for e in range(n_chip):
+            columns = block((chip + e) % n_chip, 1 - core)
+            source = terms.at[:, columns] if d is None else dense.at[tok_rows(d), columns]
+            target = core_t.at[e] if d is None else core_d.at[d, e]
+            copy = remote(source, target, (core_sem.at[0, q, e], core_sem.at[1, q, e]), sibling)
+            copy.start()
+            group.append(copy)
+        core_copies.append(group)
+    for d in range(1, n_tok):
+        for k, (source, target) in enumerate(((oa, all_oa), (ib, all_ib))):
+            copy = remote(
+                source, target.at[t], (grad_sem.at[0, d - 1, k], grad_sem.at[1, d - 1, k]), toks[d]
+            )
+            copy.start()
+            tok_copies.append(copy)
+
+    def over_core(q):
+        d, group = chunks[q], []
+        for e in range(n_chip):
+            core_copies[q][e].wait_recv()
+            columns = block((chip + e) % n_chip, core)
+            if d is None:
+                value = terms[:, columns] + core_t[e]
+            else:
+                value = dense[tok_rows(d), columns] + core_d[d, e]
+            if e == 0:
+                if d is None:
+                    kept_t[...] = value
+                else:
+                    kept_d[d] = value
+                continue
+            sent, got = (send_t, recv_t) if d is None else (send_d.at[d], recv_d.at[d])
+            sent[e - 1] = value.astype(BF16)
+            copy = remote(
+                sent.at[e - 1], got.at[e - 1],
+                (chip_sem.at[0, q, e - 1], chip_sem.at[1, q, e - 1]), chips[e],
+            )
+            copy.start()
+            group.append(copy)
+        chip_copies.append(group)
+
+    def over_chips(q):
+        d = chunks[q]
+        for copy in chip_copies[q]:
+            copy.wait_recv()
+        got = recv_t if d is None else recv_d.at[d]
+        value = kept_t[...] if d is None else kept_d[d]
+        for e in range(n_chip - 1):
+            value = value + got[e].astype(F32)
+        if d is None:
+            all_t[t] = value.astype(BF16)
+            for k in range(1, n_tok):
+                copy = remote(
+                    all_t.at[t], all_t.at[t], (term_sem.at[0, k - 1], term_sem.at[1, k - 1]), toks[k]
+                )
+                copy.start()
+                tok_copies.append(copy)
+        elif d == 0:
+            kept_d[0] = value
+        else:
+            tok_send[d - 1] = value.astype(BF16)
+            copy = remote(
+                tok_send.at[d - 1], tok_recv.at[d - 1],
+                (tok_sem.at[0, d - 1], tok_sem.at[1, d - 1]), toks[d],
+            )
+            copy.start()
+            tok_copies.append(copy)
+
+    over_core(0)
+    for q in range(1, n_tok + 1):
+        over_core(q)
+        over_chips(q - 1)
+    all_oa[t] = oa[...]
+    all_ib[t] = ib[...]
+    over_chips(n_tok)
+    for copy in tok_copies:
+        copy.wait_recv()
+    for k in range(n_tok):
+        oa_out[pl.ds(k * width, width), :] = all_oa[k].astype(F32)
+        ib_out[:, pl.ds(k * width, width)] = all_ib[k].astype(F32)
+    value = all_t[0].astype(F32)
+    for k in range(1, n_tok):
+        value = value + all_t[k].astype(F32)
+    terms_out[...] = value
+    value = kept_d[0]
+    for d in range(1, n_tok):
+        value = value + tok_recv[d - 1].astype(F32)
+    dx_out[...] = value
+    for group in core_copies + chip_copies + [tok_copies]:
+        for copy in group:
+            copy.wait_send()
+
+
+def reduce_outputs(dense, terms, oa, ib):
     n_tok, n_hid = lax.axis_size("tok"), lax.axis_size("hid")
-    stacked = jnp.concatenate([dense, terms], axis=0).astype(BF16)
-    split = lax.all_to_all(
-        stacked.reshape(stacked.shape[0], n_hid, -1).transpose(1, 0, 2),
-        "hid", split_axis=0, concat_axis=0, tiled=True,
-    )
-    over_hid = jnp.sum(split.astype(F32), axis=0).astype(BF16)
-    count = dense.shape[0]
-    mine = over_hid[:count].reshape(n_tok, count // n_tok, -1)
-    shared = jnp.broadcast_to(over_hid[count:], (n_tok,) + over_hid[count:].shape)
-    over_tok = lax.all_to_all(
-        jnp.concatenate([mine, shared], axis=1), "tok", split_axis=0, concat_axis=0, tiled=True
-    )
-    total = jnp.sum(over_tok.astype(F32), axis=0)
-    return total[: count // n_tok], total[count // n_tok :]
+    n_chip = n_hid // 2
+    rows, cols = dense.shape[0] // n_tok, dense.shape[1] // n_hid
+    count = terms.shape[0]
+    width, rank = oa.shape
+    sems = pltpu.SemaphoreType.DMA
+    vmem = pl.BlockSpec(memory_space=pltpu.VMEM)
+    return pl.pallas_call(
+        functools.partial(reduce_kernel, n_tok, n_hid),
+        out_shape=(
+            jax.ShapeDtypeStruct((rows, cols), F32),
+            jax.ShapeDtypeStruct((count, cols), F32),
+            jax.ShapeDtypeStruct((n_tok * width, rank), F32),
+            jax.ShapeDtypeStruct((rank, n_tok * width), F32),
+        ),
+        in_specs=[vmem] * 4,
+        out_specs=(vmem,) * 4,
+        scratch_shapes=[
+            pltpu.VMEM((n_tok, n_chip, rows, cols), F32),
+            pltpu.VMEM((n_chip, count, cols), F32),
+            pltpu.VMEM((n_tok, n_chip - 1, rows, cols), BF16),
+            pltpu.VMEM((n_chip - 1, count, cols), BF16),
+            pltpu.VMEM((n_tok, n_chip - 1, rows, cols), BF16),
+            pltpu.VMEM((n_chip - 1, count, cols), BF16),
+            pltpu.VMEM((n_tok, rows, cols), F32),
+            pltpu.VMEM((count, cols), F32),
+            pltpu.VMEM((n_tok - 1, rows, cols), BF16),
+            pltpu.VMEM((n_tok - 1, rows, cols), BF16),
+            pltpu.VMEM((n_tok, count, cols), BF16),
+            pltpu.VMEM((n_tok, width, rank), BF16),
+            pltpu.VMEM((n_tok, rank, width), BF16),
+            sems((2, n_tok + 1, n_chip)),
+            sems((2, n_tok + 1, n_chip - 1)),
+            sems((2, n_tok - 1)),
+            sems((2, n_tok - 1)),
+            sems((2, n_tok - 1, 2)),
+        ],
+        compiler_params=pltpu.CompilerParams(
+            collective_id=1, has_side_effects=True, vmem_limit_bytes=56 * 1024 * 1024
+        ),
+    )(dense, terms, oa, ib)
 
 
 def local(tokens, cotangent, frozen_in, frozen_out, in_a, in_b, out_a, out_b):
@@ -88,8 +248,6 @@
     oa = scale * (oa[:, :rank] + oa[:, rank:])
     ib = dot(low_in, grad_pre, ((0,), (0,)))
     ib = scale * (ib[:rank] + ib[rank:])
-    grad_out_a = lax.all_gather(oa.astype(BF16), "tok", axis=0, tiled=True).astype(F32)
-    grad_in_b = lax.all_gather(ib.astype(BF16), "tok", axis=1, tiled=True).astype(F32)
     rank_out = halves(dot(act, first, ((1,), (0,))))
     rank_back = halves(dot(grad_pre, second, ((1,), (1,))))
     dense = dot(grad_pre, w_in, ((1,), (1,))) + dot(
@@ -100,7 +258,9 @@
     terms = scale * jnp.concatenate(
         [out_term[:rank] + out_term[rank:], in_term[:rank] + in_term[rank:]], axis=0
     )
-    input_gradient, total = reduce_outputs(dense, terms)
+    input_gradient, total, grad_out_a, grad_in_b = reduce_outputs(
+        dense, terms, oa.astype(BF16), ib.astype(BF16)
+    )
     return (input_gradient, total[rank:].T, grad_in_b, grad_out_a, total[:rank])
 
 

time: 268 us -> 199 us (0.74)
  waiting for transfers between devices: 120 us -> 66.7 us
  Pallas kernels: 0 us -> 48.3 us
  blocking collectives: 53.6 us -> 10.6 us
  matrix products: 43.3 us -> 32.9 us
  starting transfers between devices: 16 us -> 7.14 us
  other arithmetic: 13.7 us -> 7.02 us
  local copies, waits for them, and re-layouts: 6.09 us -> 11.7 us
    all_to_all x2 -> x0, waiting for transfers between devices: 53.2 us -> none  [the longest x1 53.2 us: reduce_outputs(): lax.all_to_all(stacked.reshape(stacked.shape[0], n_hid, -1).transpose(1,...]
    pallas_call x0 -> x1, Pallas kernels: none -> 48.3 us  [reduce_outputs(): pl.pallas_call(functools.partial(reduce_kernel, n_tok, n_hid), out_shape=...]
    all_gather x2 -> x0, blocking collectives: 43.1 us -> none  [the longest x1 27.8 us: local(): lax.all_gather(ib.astype(BF16), 'tok', axis=1, tiled=True).astype(F32)]
    dot_general x14, matrix products: 43.3 us -> 32.9 us  [dot(): lax.dot_general(left, right, (dims, ((), ())), preferred_element_type=F32)]
    all_to_all x2 -> x0, starting transfers between devices: 8.85 us -> none  [the longest x1 4.85 us: reduce_outputs(): lax.all_to_all(stacked.reshape(stacked.shape[0], n_hid, -1).transpose(1,...]
    unnamed x49 -> x21, local copies, waits for them, and re-layouts: 3.09 us -> 8.3 us
    reduce_sum x2 -> x0, other arithmetic: 3.32 us -> none  [the longest x1 3.21 us: reduce_outputs(): over_hid = jnp.sum(split.astype(F32), axis=0).astype(BF16)]
  transfers between devices with their start and end apart: 6 -> 4, of which waited for: 4 -> 3; matrix products, arithmetic and copies ran while one was open for 5% -> 3% of each run, Pallas kernels for 0% -> 0%
where the time goes in v2:
time: 199 us
  waiting for transfers between devices  66.7 us (34%)
  Pallas kernels  48.3 us (24%)
  matrix products  32.9 us (17%)
  between operations  14.3 us (7%)
  local copies, waits for them, and re-layouts  11.7 us (6%)
  blocking collectives  10.6 us (5%)
  starting transfers between devices  7.14 us (4%)
  other arithmetic  7.02 us (4%)
    pallas_call x1, Pallas kernels, reduce_outputs(): pl.pallas_call(functools.partial(reduce_kernel, n_tok, n_hid), out_shape=...  48.3 us
    dot_general x14, matrix products, dot(): lax.dot_general(left, right, (dims, ((), ())), preferred_element_type=F32)  32.9 us
    all_gather x1, waiting for transfers between devices, gather_inputs(): lax.all_gather(jnp.stack([tokens, cotangent]), 'tok', axis=1, tiled=True)  31.8 us
    all_to_all x1, waiting for transfers between devices, gather_inputs(): lax.all_to_all(frozen_out, 'tok', split_axis=0, concat_axis=1, tiled=True)  24.2 us
    all_to_all x1, waiting for transfers between devices, gather_inputs(): lax.all_to_all(frozen_in, 'tok', split_axis=1, concat_axis=0, tiled=True)  10.7 us
    all_gather x1, blocking collectives, gather_inputs(): in_a_full = lax.all_gather(in_a, 'hid', axis=0, tiled=True)  10.6 us
    unnamed x21, local copies, waits for them, and re-layouts  8.3 us
  transfers between devices with their start and end apart: 4, of which 3 were waited for; matrix products, arithmetic and copies ran while one was open for 3% of the time, Pallas kernels for 0%

profile of v2, /device:TPU:0, one launch (start us, length us, event | category | flops | bytes accessed | tf_op | source)
XLA Modules:
  0.0 198.6 jit_solution(1530992352501201894)
XLA Ops:
  7.2 0.0 copy-start
  7.2 0.0 copy-start.1
  7.2 0.0 copy-start.5
  7.2 0.0 all-gather.3.cloned.1.call-start
  7.2 1.8 pad_maximum_fusion.9
  9.0 0.0 all-gather.3.cloned.1.call-update
  9.1 0.0 all-gather.5.cloned.1.call-start
  9.1 31.8 %all-gather.3.cloned.1.call-done = bf16[2,2048,128]{2,1,0:T(8,128)(2,1)} async-done(((bf16[2,512,128]{2,1,0:T(8,128)(2,1)}), bf16[2,2048,128]{2,1,0:T(8,128)(2,1)}) %all-gather.3.cloned.1.call-update) | async-done | bytes 1048592 | tf_op jit(solution)/shard_map/all_gather | solution.py:41
  40.9 0.0 all-gather.5.cloned.1.call-update
  40.9 3.5 %all-to-all-start = ((bf16[4,512,256]{2,1,0:T(8,128)(2,1)}), bf16[4,512,256]{2,1,0:T(8,128)(2,1)S(1)}, u32[]{:S(2)}, u32[]{:S(2)}) async-start(bf16[4,512,256]{2,1,0:T(8,128)(2,1)} %bitcast.34), calls=%async_computation | async-start | bytes 2097152 | tf_op jit(solution)/shard_map/all_to_all | solution.py:45
  44.5 0.0 copy-done.1
  44.5 1.3 copy.16
  45.8 24.2 %all-to-all-done = bf16[4,512,256]{2,1,0:T(8,128)(2,1)S(1)} async-done(((bf16[4,512,256]{2,1,0:T(8,128)(2,1)}), bf16[4,512,256]{2,1,0:T(8,128)(2,1)S(1)}, u32[]{:S(2)}, u32[]{:S(2)}) %all-to-all-start) | async-done | bytes 1048608 | tf_op jit(solution)/shard_map/all_to_all | solution.py:45
  69.9 3.5 %all-to-all-start.1 = ((bf16[256,4,512]{0,2,1:T(8,128)(2,1)}), bf16[256,4,512]{0,2,1:T(8,128)(2,1)S(1)}, u32[]{:S(2)}, u32[]{:S(2)}) async-start(bf16[256,4,512]{0,2,1:T(8,128)(2,1)} %bitcast.7), calls=%async_computation.1 | async-start | bytes 2097152 | tf_op jit(solution)/shard_map/all_to_all | solution.py:44
  73.5 0.0 copy-done.5
  73.5 10.6 %all_gather.11 = bf16[1024,128]{1,0:T(8,128)(2,1)S(1)} all-gather(bf16[128,128]{1,0:T(8,128)(2,1)S(1)} %copy-done.5), channel_id=1, replica_groups=mesh['tok'=4,'hid'=8] {'hid'}, dimensions={0}, use_global_device_ids=true | all-gather | bytes 294912 | tf_op jit(solution)/shard_map/all_gather | solution.py:43
  84.1 0.0 copy-start.3
  84.1 1.0 dynamic-slice_multiply_fusion
  85.1 1.6 dynamic-slice_multiply_fusion.1
  86.7 1.3 copy.15
  88.0 10.7 %all-to-all-done.1 = bf16[256,4,512]{0,2,1:T(8,128)(2,1)S(1)} async-done(((bf16[256,4,512]{0,2,1:T(8,128)(2,1)}), bf16[256,4,512]{0,2,1:T(8,128)(2,1)S(1)}, u32[]{:S(2)}, u32[]{:S(2)}) %all-to-all-start.1) | async-done | bytes 1048608 | tf_op jit(solution)/shard_map/all_to_all | solution.py:44
  98.7 0.0 copy-done.3
  98.7 0.5 copy.17
  99.3 0.0 all-gather.5.cloned.1.call-done
  99.3 3.7 %reduce-precision_convert_fusion.2 = (bf16[2048,128]{0,1:T(8,128)(2,1)S(1)}, bf16[2048,128]{0,1:T(8,128)(2,1)S(1)}) fusion(bf16[1024,128]{1,0:T(8,128)(2,1)} %copy-done.3, bf16[2,2048,1024]{2,1,0:T(8,128)(2,1)} %all-gather.5.cloned.1.call-done), kind=kOutput, calls=%fused_computation.25 | convolution fusion | flops 537919488 | bytes 5505024 | tf_op jit(solution)/shard_map/dot_general | solution.py:35
  103.0 4.6 %fusion.12 = f32[2048,512]{1,0:T(8,128)S(1)} fusion(bf16[1024,512]{1,0:T(8,128)(2,1)S(1)} %bitcast.35, bf16[2,2048,1024]{2,1,0:T(8,128)(2,1)} %all-gather.5.cloned.1.call-done), kind=kOutput, calls=%fused_computation.19 | convolution fusion | flops 2147483648 | bytes 9437184 | tf_op jit(solution)/shard_map/dot_general | solution.py:35
  107.6 0.0 slice-start
  107.6 0.8 convolution_add_fusion.1
  108.4 0.0 slice-start.1
  108.4 2.9 %reduce-precision_convert_fusion = (bf16[2048,128]{0,1:T(8,128)(2,1)S(1)}, bf16[2048,128]{0,1:T(8,128)(2,1)S(1)}) fusion(bf16[2048,128]{1,0:T(8,128)(2,1)} %param.14, s32[]{:T(128)S(6)} %select_n.4, f32[2048,512]{1,0:T(8,128)S(1)} %convolution_add_fusion.1), kind=kOutput, calls=%fused_computation.21 | convolution fusion | flops 278921216 | bytes 5373956 | tf_op jit(solution)/shard_map/dot_general | solution.py:35
  111.4 0.0 copy-done
  111.4 0.0 slice-done
  111.4 0.0 slice-done.1
  111.4 1.5 reduce-precision_convert_fusion.3
  113.0 0.0 copy-start.2
  113.0 1.5 fusion.21
  114.5 0.0 copy-done.2
  114.5 0.0 copy-start.4
  114.5 2.4 %fusion.9 = f32[2048,512]{1,0:T(8,128)S(1)} fusion(bf16[512,1024]{0,1:T(8,128)(2,1)S(1)} %bitcast.37, bf16[2,2048,1024]{2,1,0:T(8,128)(2,1)S(1)} %bitcast.41), kind=kOutput, calls=%fused_computation.16 | convolution fusion | flops 2147483648 | bytes 9437184 | tf_op jit(solution)/shard_map/dot_general | solution.py:35
  117.0 0.0 copy-done.4
  117.0 3.4 %fusion.6 = bf16[2048,512]{1,0:T(8,128)(2,1)S(1)} fusion(f32[2048,512]{1,0:T(8,128)S(1)} %convolution_add_fusion.1, f32[2048,512]{1,0:T(8,128)S(1)} %fusion.9, bf16[2048,128]{0,1:T(8,128)(2,1)S(1)} %get-tuple-element.33, bf16[2048,128]{0,1:T(8,128)(2,1)S(1)} %get-tuple-element.32, bf16[512,128]{1,0:T(8,128)(2,1)S(1)} %copy-done.4), kind=kOutput, calls=%fused_computation.9 | convolution fusion | flops 560463872 | bytes 11665408 | tf_op jit(solution)/shard_map/dot_general | solution.py:35
  120.4 0.7 fusion.20
  121.1 1.7 reduce-precision_convert_fusion.1
  122.8 2.4 %fusion.49 = f32[2048,1024]{1,0:T(8,128)S(1)} fusion(bf16[2048,512]{1,0:T(8,128)(2,1)S(1)} %fusion.6, bf16[1024,512]{1,0:T(8,128)(2,1)S(1)} %bitcast.36), kind=kOutput, calls=%fused_computation.77 | convolution fusion | flops 2147483648 | bytes 11534336 | tf_op jit(solution)/shard_map/dot_general | solution.py:35
  125.2 0.7 fusion.26.ib
  125.9 0.7 fusion.28.oa
  126.6 1.3 fusion.7
  127.9 1.3 fusion.10
  129.2 0.1 slice_add_fusion
  129.3 1.1 maximum_multiply_fusion.terms
  130.4 4.6 %convolution_add_fusion.dense = f32[2048,1024]{1,0:T(8,128)} fusion(f32[2048,1024]{1,0:T(8,128)S(1)} %fusion.49, bf16[2048,128]{0,1:T(8,128)(2,1)S(1)} %get-tuple-element.31, bf16[2048,128]{0,1:T(8,128)(2,1)S(1)} %get-tuple-element.30, bf16[1024,128]{1,0:T(8,128)(2,1)S(1)} %broadcast_multiply_fusion), kind=kOutput, calls=%fused_computation.2 | convolution fusion | flops 1078984704 | bytes 18087936 | tf_op jit(solution)/shard_map/dot_general | solution.py:35
  135.0 48.3 %shard_map.119 = (f32[512,128]{1,0:T(8,128)}, f32[256,128]{1,0:T(8,128)}, f32[2048,128]{1,0:T(8,128)}, f32[128,2048]{1,0:T(8,128)}) custom-call(f32[2048,1024]{1,0:T(8,128)} %convolution_add_fusion.dense, f32[256,1024]{1,0:T(8,128)} %maximum_multiply_fusion.terms, bf16[512,128]{1,0:T(8,128)(2,1)} %fusion.28.oa, bf16[128,512]{1,0:T(8,128)(2,1)} %fusion.26.ib), custom_call_target="tpu_custom_call" | custom-call | tf_op jit(solution)/shard_map/pallas_call | solution.py:188
  183.2 1.5 fusion.48
  184.8 0.7 copy.18
  185.5 1.7 copy.22
  187.2 2.3 %copy.23 = f32[128,2048]{1,0:T(8,128)} copy(f32[128,2048]{1,0:T(8,128)} %get-tuple-element.47) | data formatting | bytes 2097152
  189.5 2.3 %copy.24 = f32[2048,128]{1,0:T(8,128)} copy(f32[2048,128]{1,0:T(8,128)} %get-tuple-element.48) | data formatting | bytes 2097152
  (2 shorter events, 0.0 us)
Async XLA Ops:
  7.2 104.2 %copy-start = (bf16[128,1024]{1,0:T(8,128)(2,1)S(1)}, bf16[128,1024]{1,0:T(8,128)(2,1)}, u32[]{:S(2)}) copy-start(bf16[128,1024]{1,0:T(8,128)(2,1)} %param.15) | copy-start | bytes 786436
  7.2 37.3 %copy-start.1 = (bf16[256,2048]{1,0:T(8,128)(2,1)S(1)}, bf16[256,2048]{1,0:T(8,128)(2,1)}, u32[]{:S(2)}) copy-start(bf16[256,2048]{1,0:T(8,128)(2,1)} %param.10) | copy-start | bytes 3145732
  7.2 66.3 %copy-start.5 = (bf16[128,128]{1,0:T(8,128)(2,1)S(1)}, bf16[128,128]{1,0:T(8,128)(2,1)}, u32[]{:S(2)}) copy-start(bf16[128,128]{1,0:T(8,128)(2,1)} %param.12) | copy-start | bytes 98308
  7.2 33.7 %all-gather.3.cloned.1.call-start = ((), (), s32[]{:S(2)}) async-start(), calls=%async_computation.2 | async-start | bytes 1310720 | tf_op jit(solution)/shard_map/all_gather | solution.py:41
  9.1 90.2 %all-gather.5.cloned.1.call-start = ((), (), s32[]{:S(2)}) async-start(), calls=%async_computation.3 | async-start | bytes 9437184 | tf_op jit(solution)/shard_map/all_gather | solution.py:42
  40.9 29.0 %all-to-all-start = ((bf16[4,512,256]{2,1,0:T(8,128)(2,1)}), bf16[4,512,256]{2,1,0:T(8,128)(2,1)S(1)}, u32[]{:S(2)}, u32[]{:S(2)}) async-start(bf16[4,512,256]{2,1,0:T(8,128)(2,1)} %bitcast.34), calls=%async_computation | async-start | bytes 2097152 | tf_op jit(solution)/shard_map/all_to_all | solution.py:45
  69.9 28.8 %all-to-all-start.1 = ((bf16[256,4,512]{0,2,1:T(8,128)(2,1)}), bf16[256,4,512]{0,2,1:T(8,128)(2,1)S(1)}, u32[]{:S(2)}, u32[]{:S(2)}) async-start(bf16[256,4,512]{0,2,1:T(8,128)(2,1)} %bitcast.7), calls=%async_computation.1 | async-start | bytes 2097152 | tf_op jit(solution)/shard_map/all_to_all | solution.py:44
  84.1 14.7 %copy-start.3 = (bf16[1024,128]{1,0:T(8,128)(2,1)}, bf16[1024,128]{1,0:T(8,128)(2,1)S(1)}, u32[]{:S(2)}) copy-start(bf16[1024,128]{1,0:T(8,128)(2,1)S(1)} %all_gather.11) | copy-start | bytes 786436
  107.6 3.8 %slice-start = ((s8[8388608]{0:T(1024)(128)(4,1)}), s8[4194304]{0:T(1024)(128)(4,1)S(1)}, s32[]{:S(2)}) async-start(s8[8388608]{0:T(1024)(128)(4,1)} %bitcast.40), calls=%async_computation.4 | async-start | bytes 8388608
  108.4 3.0 %slice-start.1 = ((s8[8388608]{0:T(1024)(128)(4,1)}), s8[4194304]{0:T(1024)(128)(4,1)S(1)}, s32[]{:S(2)}) async-start(s8[8388608]{0:T(1024)(128)(4,1)} %bitcast.40), calls=%async_computation.5 | async-start | bytes 8388608
  113.0 1.6 copy-start.2
  114.5 2.4 %copy-start.4 = (bf16[512,128]{1,0:T(8,128)(2,1)S(1)}, bf16[512,128]{1,0:T(8,128)(2,1)}, u32[]{:S(2)}) copy-start(bf16[512,128]{1,0:T(8,128)(2,1)} %dynamic-slice_multiply_fusion.1) | copy-start | bytes 393220
Sparse Core Ops, SparseCore 0:
  10.2 30.6 all-gather.2
  42.8 56.2 all-gather.4

commit v3 on v2

--- a/solution.py
+++ b/solution.py
@@ -35,15 +35,161 @@
     return lax.dot_general(left, right, (dims, ((), ())), preferred_element_type=F32)
 
 
+def gather_kernel(
+    n_tok, n_hid, tokens, cotangent, w_in, w_out, in_a,
+    x, c, full_in, full_out, full_a,
+    tok_sem, chip_sem, core_sem, first_sem, first_core_sem, own_sem,
+):
+    t, h = lax.axis_index("tok"), lax.axis_index("hid")
+    n_chip = n_hid // 2
+    chip, core = h // 2, h % 2
+    rows, cols = tokens.shape
+    depth = w_in.shape[0]
+    width = full_in.shape[1]
+
+    def remote(source, target, sems, where):
+        copy = pltpu.make_async_remote_copy(
+            src_ref=source, dst_ref=target, send_sem=sems[0], recv_sem=sems[1],
+            device_id=where, device_id_type=pl.DeviceIdType.MESH,
+        )
+        copy.start()
+        return copy
+
+    def pair(sems, *where):
+        return sems.at[(0,) + where], sems.at[(1,) + where]
+
+    sibling = (t, 2 * chip + 1 - core)
+    chips = [(t, 2 * ((chip + e) % n_chip) + core) for e in range(n_chip)]
+    toks = [((t + d) % n_tok, h) for d in range(n_tok)]
+    barrier = pltpu.get_barrier_semaphore()
+    for where in [sibling] + chips[1:] + toks[1:]:
+        pl.semaphore_signal(barrier, inc=1, device_id=where, device_id_type=pl.DeviceIdType.MESH)
+    pl.semaphore_wait(barrier, n_chip + n_tok - 1)
+
+    def part(array, d, e):
+        at_row = pl.multiple_of(((t + n_tok - d) % n_tok) * rows, rows)
+        at_col = pl.multiple_of((2 * ((chip + n_chip - e) % n_chip) + core) * cols, cols)
+        return array.at[pl.ds(at_row, rows), pl.ds(at_col, cols)]
+
+    def first_part(e):
+        at = pl.multiple_of((2 * ((chip + n_chip - e) % n_chip) + core) * cols, cols)
+        return full_a.at[pl.ds(at, cols), :]
+
+    both = ((tokens, x), (cotangent, c))
+    sent, from_tok, from_chip, from_core, weights = [], [], [], [], []
+    for d in range(1, n_tok):
+        from_tok.append([
+            remote(own, part(whole, 0, 0), pair(tok_sem, d - 1, k), toks[d])
+            for k, (own, whole) in enumerate(both)
+        ])
+
+    def to_chips(d, blocks):
+        from_chip.append([
+            [
+                remote(blocks[k], part(both[k][1], d, 0), pair(chip_sem, d, e - 1, k), chips[e])
+                for k in range(2)
+            ]
+            for e in range(1, n_chip)
+        ])
+
+    def to_core(d, e, blocks):
+        for k in range(2):
+            from_core.append(
+                remote(blocks[k], part(both[k][1], d, e), pair(core_sem, d, e, k), sibling)
+            )
+
+    to_chips(0, (tokens, cotangent))
+    firsts = [
+        remote(in_a, first_part(0), pair(first_sem, e - 1), chips[e]) for e in range(1, n_chip)
+    ]
+    to_core(0, 0, (tokens, cotangent))
+    from_core.append(remote(in_a, first_part(0), pair(first_core_sem, 0), sibling))
+    for d in range(1, n_tok):
+        at = pl.multiple_of(((t + d) % n_tok) * width, width)
+        depths = pl.ds(pl.multiple_of(t * depth, depth), depth)
+        weights.append(remote(
+            w_in.at[:, pl.ds(at, width)], full_in.at[depths, :], pair(tok_sem, d - 1, 2), toks[d]
+        ))
+        weights.append(remote(
+            w_out.at[pl.ds(at, width), :], full_out.at[:, depths], pair(tok_sem, d - 1, 3), toks[d]
+        ))
+    at = pl.multiple_of(t * width, width)
+    depths = pl.ds(pl.multiple_of(t * depth, depth), depth)
+    own = [
+        (tokens, part(x, 0, 0)),
+        (cotangent, part(c, 0, 0)),
+        (w_in.at[:, pl.ds(at, width)], full_in.at[depths, :]),
+        (w_out.at[pl.ds(at, width), :], full_out.at[:, depths]),
+        (in_a, first_part(0)),
+    ]
+    own = [
+        pltpu.make_async_copy(source, target, own_sem.at[k])
+        for k, (source, target) in enumerate(own)
+    ]
+    for copy in own:
+        copy.start()
+
+    def pass_on(d):
+        for e in range(1, n_chip):
+            for copy in from_chip[d][e - 1]:
+                copy.wait_recv()
+            to_core(d, e, (part(x, d, e), part(c, d, e)))
+
+    for d in range(1, n_tok):
+        for copy in from_tok[d - 1]:
+            copy.wait_recv()
+        blocks = (part(x, d, 0), part(c, d, 0))
+        to_chips(d, blocks)
+        to_core(d, 0, blocks)
+        pass_on(d - 1)
+    for e in range(1, n_chip):
+        firsts[e - 1].wait_recv()
+        from_core.append(remote(first_part(e), first_part(e), pair(first_core_sem, e), sibling))
+    pass_on(n_tok - 1)
+    for copy in from_core + weights:
+        copy.wait_recv()
+    for copy in own:
+        copy.wait()
+    for group in from_tok + [firsts, from_core, weights]:
+        for copy in group:
+            copy.wait_send()
+    for groups in from_chip:
+        for group in groups:
+            for copy in group:
+                copy.wait_send()
+
+
 def gather_inputs(tokens, cotangent, frozen_in, frozen_out, in_a):
-    rows, rank = tokens.shape[0], in_a.shape[1]
-    n_tok = lax.axis_size("tok")
-    both = lax.all_gather(jnp.stack([tokens, cotangent]), "tok", axis=1, tiled=True)
-    both = lax.all_gather(both, "hid", axis=2, tiled=True)
-    in_a_full = lax.all_gather(in_a, "hid", axis=0, tiled=True)
-    w_in = lax.all_to_all(frozen_in, "tok", split_axis=1, concat_axis=0, tiled=True)
-    w_out = lax.all_to_all(frozen_out, "tok", split_axis=0, concat_axis=1, tiled=True)
-    return both[0], both[1], w_in, w_out, in_a_full
+    n_tok, n_hid = lax.axis_size("tok"), lax.axis_size("hid")
+    n_chip = n_hid // 2
+    count, features = tokens.shape[0] * n_tok, tokens.shape[1] * n_hid
+    width = frozen_in.shape[1] // n_tok
+    sems = pltpu.SemaphoreType.DMA
+    vmem = pl.BlockSpec(memory_space=pltpu.VMEM)
+    whole = pl.BlockSpec(memory_space=pl.ANY)
+    return pl.pallas_call(
+        functools.partial(gather_kernel, n_tok, n_hid),
+        out_shape=(
+            jax.ShapeDtypeStruct((count, features), BF16),
+            jax.ShapeDtypeStruct((count, features), BF16),
+            jax.ShapeDtypeStruct((features, width), BF16),
+            jax.ShapeDtypeStruct((width, features), BF16),
+            jax.ShapeDtypeStruct((features, in_a.shape[1]), BF16),
+        ),
+        in_specs=[vmem] * 5,
+        out_specs=(whole,) * 5,
+        scratch_shapes=[
+            sems((2, n_tok - 1, 4)),
+            sems((2, n_tok, n_chip - 1, 2)),
+            sems((2, n_tok, n_chip, 2)),
+            sems((2, n_chip - 1)),
+            sems((2, n_chip)),
+            sems((5,)),
+        ],
+        compiler_params=pltpu.CompilerParams(
+            collective_id=2, has_side_effects=True, vmem_limit_bytes=56 * 1024 * 1024
+        ),
+    )(tokens, cotangent, frozen_in, frozen_out, in_a)
 
 
 def reduce_kernel(

time: 199 us -> 170 us (0.85)
  Pallas kernels: 48.3 us -> 124 us
  waiting for transfers between devices: 66.7 us -> 0 us
  between operations: 14.3 us -> 0.84 us
  blocking collectives: 10.6 us -> 0 us
  starting transfers between devices: 7.14 us -> 0 us
  local copies, waits for them, and re-layouts: 11.7 us -> 8.51 us
  matrix products: 32.9 us -> 30.4 us
    pallas_call x0 -> x1, Pallas kernels: none -> 67.5 us  [gather_inputs(): pl.pallas_call(functools.partial(gather_kernel, n_tok, n_hid), out_shape=...]
    all_to_all x2 -> x0, waiting for transfers between devices: 34.9 us -> none  [the longest x1 24.2 us: gather_inputs(): lax.all_to_all(frozen_out, 'tok', split_axis=0, concat_axis=1, tiled=True)]
    all_gather x2 -> x0, waiting for transfers between devices: 31.8 us -> none  [the longest x1 31.8 us: gather_inputs(): lax.all_gather(jnp.stack([tokens, cotangent]), 'tok', axis=1, tiled=True)]
    all_gather x1 -> x0, blocking collectives: 10.6 us -> none  [gather_inputs(): in_a_full = lax.all_gather(in_a, 'hid', axis=0, tiled=True)]
    pallas_call x1, Pallas kernels: 48.3 us -> 56.2 us  [reduce_outputs(): pl.pallas_call(functools.partial(reduce_kernel, n_tok, n_hid), out_shape=...]
    all_to_all x2 -> x0, starting transfers between devices: 7.06 us -> none  [the longest x1 3.53 us: gather_inputs(): lax.all_to_all(frozen_in, 'tok', split_axis=1, concat_axis=0, tiled=True)]
    dot_general x14, matrix products: 32.9 us -> 30.4 us  [dot(): lax.dot_general(left, right, (dims, ((), ())), preferred_element_type=F32)]
    unnamed x21 -> x14, local copies, waits for them, and re-layouts: 8.3 us -> 7 us
  transfers between devices with their start and end apart: 4 -> 0, of which waited for: 3 -> 0; matrix products, arithmetic and copies ran while one was open for 3% -> 0% of each run, Pallas kernels for 0% -> 0%
where the time goes in v3:
time: 170 us; the launch traced here: 169 us
  Pallas kernels  124 us (73%)
  matrix products  30.4 us (18%)
  local copies, waits for them, and re-layouts  8.51 us (5%)
  other arithmetic  5.68 us (3%)
    pallas_call x1, Pallas kernels, gather_inputs(): pl.pallas_call(functools.partial(gather_kernel, n_tok, n_hid), out_shape=...  67.5 us
    pallas_call x1, Pallas kernels, reduce_outputs(): pl.pallas_call(functools.partial(reduce_kernel, n_tok, n_hid), out_shape=...  56.2 us
    dot_general x14, matrix products, dot(): lax.dot_general(left, right, (dims, ((), ())), preferred_element_type=F32)  30.4 us
    unnamed x14, local copies, waits for them, and re-layouts  7 us

profile of v3, /device:TPU:0, one launch (start us, length us, event | category | flops | bytes accessed | tf_op | source)
XLA Modules:
  0.0 169.2 jit_solution(3461243369972474223)
XLA Ops:
  0.6 0.0 copy-start
  0.7 1.0 dynamic-slice_multiply_fusion
  1.6 0.9 dynamic-slice_multiply_fusion.1
  2.6 67.5 %shard_map.119 = (bf16[2048,1024]{1,0:T(8,128)(2,1)}, bf16[2048,1024]{1,0:T(8,128)(2,1)}, bf16[1024,512]{1,0:T(8,128)(2,1)}, bf16[512,1024]{1,0:T(8,128)(2,1)}, bf16[1024,128]{1,0:T(8,128)(2,1)}) custom-call(bf16[512,128]{1,0:T(8,128)(2,1)} %tokens.1, bf16[512,128]{1,0:T(8,128)(2,1)} %cotangent.1, bf16[256,2048]{1,0:T(8,128)(2,1)} %w_in.1, ...), custom_call_target="tpu_custom_call" | custom-call | tf_op jit(solution)/shard_map/pallas_call | solution.py:170
  70.1 0.0 copy-start.2
  70.1 1.1 broadcast_multiply_fusion
  71.2 3.9 %reduce-precision_convert_fusion.2 = (bf16[2048,128]{0,1:T(8,128)(2,1)S(1)}, bf16[2048,128]{0,1:T(8,128)(2,1)S(1)}) fusion(bf16[2048,1024]{1,0:T(8,128)(2,1)} %get-tuple-element.16, bf16[1024,128]{1,0:T(8,128)(2,1)} %get-tuple-element.18), kind=kOutput, calls=%fused_computation.17 | convolution fusion | flops 537919488 | bytes 5505024 | tf_op jit(solution)/shard_map/dot_general | solution.py:35
  75.2 0.0 copy-start.4
  75.2 0.0 copy-done
  75.2 0.0 copy-done.2
  75.2 1.5 reduce-precision_convert_fusion.3
  76.7 0.0 copy-done.4
  76.8 0.0 copy-start.1
  76.8 0.0 copy-start.3
  76.8 2.4 %fusion.45 = f32[2048,512]{1,0:T(8,128)S(1)} fusion(bf16[2048,1024]{1,0:T(8,128)(2,1)S(1)} %copy-done.2, bf16[512,1024]{1,0:T(8,128)(2,1)S(1)} %copy-done.4), kind=kOutput, calls=%fused_computation.70 | convolution fusion | flops 2147483648 | bytes 9437184 | tf_op jit(solution)/shard_map/dot_general | solution.py:35
  79.2 0.0 copy-done.1
  79.2 0.0 copy-done.3
  79.2 2.4 %fusion.46 = f32[2048,512]{1,0:T(8,128)S(1)} fusion(bf16[2048,1024]{1,0:T(8,128)(2,1)S(1)} %copy-done.1, bf16[1024,512]{1,0:T(8,128)(2,1)S(1)} %copy-done.3), kind=kOutput, calls=%fused_computation.71 | convolution fusion | flops 2147483648 | bytes 9437184 | tf_op jit(solution)/shard_map/dot_general | solution.py:35
  81.6 0.8 convolution_add_fusion.1
  82.4 3.4 %fusion.6 = bf16[2048,512]{1,0:T(8,128)(2,1)S(1)} fusion(f32[2048,512]{1,0:T(8,128)S(1)} %convolution_add_fusion.1, f32[2048,512]{1,0:T(8,128)S(1)} %fusion.45, bf16[2048,128]{0,1:T(8,128)(2,1)S(1)} %get-tuple-element.33, bf16[2048,128]{0,1:T(8,128)(2,1)S(1)} %get-tuple-element.32, bf16[512,128]{1,0:T(8,128)(2,1)S(1)} %dynamic-slice_multiply_fusion.1), kind=kOutput, calls=%fused_computation.9 | convolution fusion | flops 560463872 | bytes 11665408 | tf_op jit(solution)/shard_map/dot_general | solution.py:35
  85.8 1.5 fusion.17
  87.4 2.6 %reduce-precision_convert_fusion = (bf16[2048,128]{0,1:T(8,128)(2,1)S(1)}, bf16[2048,128]{0,1:T(8,128)(2,1)S(1)}) fusion(bf16[2048,128]{1,0:T(8,128)(2,1)} %param.14, s32[]{:T(128)S(6)} %select_n.4, f32[2048,512]{1,0:T(8,128)S(1)} %convolution_add_fusion.1), kind=kOutput, calls=%fused_computation.13 | convolution fusion | flops 278921216 | bytes 5373956 | tf_op jit(solution)/shard_map/dot_general | solution.py:35
  89.9 0.7 fusion.16
  90.6 0.7 fusion.22.ib
  91.3 0.7 fusion.24.oa
  92.0 1.3 fusion.11
  93.3 1.7 %reduce-precision_convert_fusion.1 = (bf16[2048,128]{0,1:T(8,128)(2,1)S(1)}, bf16[2048,128]{0,1:T(8,128)(2,1)S(1)}) fusion(bf16[2048,512]{1,0:T(8,128)(2,1)S(1)} %fusion.6, bf16[128,2048]{1,0:T(8,128)(2,1)} %param.13, s32[]{:T(128)S(6)} %select_n.4), kind=kOutput, calls=%fused_computation.15 | convolution fusion | flops 269484032 | bytes 3276804 | tf_op jit(solution)/shard_map/dot_general | solution.py:35
  95.1 1.3 fusion.15
  96.3 0.2 slice_add_fusion
  96.5 1.1 maximum_multiply_fusion.terms
  97.6 2.4 %fusion.47 = f32[2048,1024]{1,0:T(8,128)S(1)} fusion(bf16[2048,512]{1,0:T(8,128)(2,1)S(1)} %fusion.6, bf16[1024,512]{1,0:T(8,128)(2,1)S(1)} %copy-done.3), kind=kOutput, calls=%fused_computation.72 | convolution fusion | flops 2147483648 | bytes 11534336 | tf_op jit(solution)/shard_map/dot_general | solution.py:35
  100.0 4.5 %convolution_add_fusion.dense = f32[2048,1024]{1,0:T(8,128)} fusion(f32[2048,1024]{1,0:T(8,128)S(1)} %fusion.47, bf16[2048,128]{0,1:T(8,128)(2,1)S(1)} %get-tuple-element.31, bf16[2048,128]{0,1:T(8,128)(2,1)S(1)} %get-tuple-element.30, bf16[1024,128]{1,0:T(8,128)(2,1)S(1)} %broadcast_multiply_fusion), kind=kOutput, calls=%fused_computation.2 | convolution fusion | flops 1078984704 | bytes 18087936 | tf_op jit(solution)/shard_map/dot_general | solution.py:35
  104.5 56.2 %shard_map.120 = (f32[512,128]{1,0:T(8,128)}, f32[256,128]{1,0:T(8,128)}, f32[2048,128]{1,0:T(8,128)}, f32[128,2048]{1,0:T(8,128)}) custom-call(f32[2048,1024]{1,0:T(8,128)} %convolution_add_fusion.dense, f32[256,1024]{1,0:T(8,128)} %maximum_multiply_fusion.terms, bf16[512,128]{1,0:T(8,128)(2,1)} %fusion.24.oa, bf16[128,512]{1,0:T(8,128)(2,1)} %fusion.22.ib), custom_call_target="tpu_custom_call" | custom-call | tf_op jit(solution)/shard_map/pallas_call | solution.py:334
  160.7 1.5 fusion.44
  162.2 0.7 copy.13
  162.9 1.7 copy.17
  164.6 2.3 %copy.18 = f32[128,2048]{1,0:T(8,128)} copy(f32[128,2048]{1,0:T(8,128)} %get-tuple-element.47) | data formatting | bytes 2097152
  166.9 2.3 %copy.19 = f32[2048,128]{1,0:T(8,128)} copy(f32[2048,128]{1,0:T(8,128)} %get-tuple-element.48) | data formatting | bytes 2097152
Async XLA Ops:
  0.6 74.6 %copy-start = (bf16[128,1024]{1,0:T(8,128)(2,1)S(1)}, bf16[128,1024]{1,0:T(8,128)(2,1)}, u32[]{:S(2)}) copy-start(bf16[128,1024]{1,0:T(8,128)(2,1)} %param.15) | copy-start | bytes 786436
  70.1 5.1 %copy-start.2 = (bf16[2048,1024]{1,0:T(8,128)(2,1)S(1)}, bf16[2048,1024]{1,0:T(8,128)(2,1)}, u32[]{:S(2)}) copy-start(bf16[2048,1024]{1,0:T(8,128)(2,1)} %get-tuple-element.14) | copy-start | bytes 12582916
  75.2 1.6 copy-start.4
  76.8 2.5 %copy-start.1 = (bf16[2048,1024]{1,0:T(8,128)(2,1)S(1)}, bf16[2048,1024]{1,0:T(8,128)(2,1)}, u32[]{:S(2)}) copy-start(bf16[2048,1024]{1,0:T(8,128)(2,1)} %get-tuple-element.16) | copy-start | bytes 12582916
  76.8 2.5 %copy-start.3 = (bf16[1024,512]{1,0:T(8,128)(2,1)S(1)}, bf16[1024,512]{1,0:T(8,128)(2,1)}, u32[]{:S(2)}) copy-start(bf16[1024,512]{1,0:T(8,128)(2,1)} %get-tuple-element.17) | copy-start | bytes 3145732

commit v4 on v3

--- a/solution.py
+++ b/solution.py
@@ -194,9 +194,9 @@
 
 def reduce_kernel(
     n_tok, n_hid, dense, terms, oa, ib,
-    dx_out, terms_out, oa_out, ib_out,
+    dx_out, terms_out, all_oa, all_ib,
     core_d, core_t, send_d, send_t, recv_d, recv_t, kept_d, kept_t, tok_send, tok_recv,
-    all_t, all_oa, all_ib,
+    all_t,
     core_sem, chip_sem, tok_sem, term_sem, grad_sem,
 ):
     t, h = lax.axis_index("tok"), lax.axis_index("hid")
@@ -204,7 +204,6 @@
     chip, core = h // 2, h % 2
     rows, cols = dx_out.shape
     count = terms.shape[0]
-    width = oa.shape[0]
 
     def remote(source, target, sems, where):
         return pltpu.make_async_remote_copy(
@@ -238,13 +237,41 @@
             copy.start()
             group.append(copy)
         core_copies.append(group)
-    for d in range(1, n_tok):
-        for k, (source, target) in enumerate(((oa, all_oa), (ib, all_ib))):
-            copy = remote(
-                source, target.at[t], (grad_sem.at[0, d - 1, k], grad_sem.at[1, d - 1, k]), toks[d]
-            )
-            copy.start()
-            tok_copies.append(copy)
+    grads = ((oa, all_oa), (ib, all_ib))
+
+    def grad_copy(way, k, item):
+        at = lax.rem(t + (n_tok - k if way == 0 else k), n_tok)
+        to = lax.rem(t + (1 if way == 0 else n_tok - 1), n_tok)
+        own, whole = grads[item]
+        return remote(
+            own if k == 0 else whole.at[at], whole.at[at],
+            (grad_sem.at[0, way, k, item], grad_sem.at[1, way, k, item]), (to, h),
+        )
+
+    def each_grad(way, k, act):
+        for item in range(2):
+            act(grad_copy(way, k, item))
+
+    def sends(way, k):
+        return jnp.logical_and(t >= k, t < n_tok - 1) if way == 0 else jnp.logical_and(
+            t + k < n_tok, t > 0
+        )
+
+    def receives(way, k):
+        return t >= k + 1 if way == 0 else t + k + 1 < n_tok
+
+    def pass_grads(k):
+        for way in range(2):
+            if k > 0:
+                pl.when(receives(way, k - 1))(
+                    lambda way=way: each_grad(way, k - 1, lambda copy: copy.wait_recv())
+                )
+            if k < n_tok - 1:
+                pl.when(sends(way, k))(
+                    lambda way=way: each_grad(way, k, lambda copy: copy.start())
+                )
+
+    pass_grads(0)
 
     def over_core(q):
         d, group = chunks[q], []
@@ -302,14 +329,13 @@
     for q in range(1, n_tok + 1):
         over_core(q)
         over_chips(q - 1)
+        if q < n_tok:
+            pass_grads(q)
     all_oa[t] = oa[...]
     all_ib[t] = ib[...]
     over_chips(n_tok)
     for copy in tok_copies:
         copy.wait_recv()
-    for k in range(n_tok):
-        oa_out[pl.ds(k * width, width), :] = all_oa[k].astype(F32)
-        ib_out[:, pl.ds(k * width, width)] = all_ib[k].astype(F32)
     value = all_t[0].astype(F32)
     for k in range(1, n_tok):
         value = value + all_t[k].astype(F32)
@@ -321,6 +347,11 @@
     for group in core_copies + chip_copies + [tok_copies]:
         for copy in group:
             copy.wait_send()
+    for k in range(n_tok - 1):
+        for way in range(2):
+            pl.when(sends(way, k))(
+                lambda way=way, k=k: each_grad(way, k, lambda copy: copy.wait_send())
+            )
 
 
 def reduce_outputs(dense, terms, oa, ib):
@@ -336,8 +367,8 @@
         out_shape=(
             jax.ShapeDtypeStruct((rows, cols), F32),
             jax.ShapeDtypeStruct((count, cols), F32),
-            jax.ShapeDtypeStruct((n_tok * width, rank), F32),
-            jax.ShapeDtypeStruct((rank, n_tok * width), F32),
+            jax.ShapeDtypeStruct((n_tok, width, rank), BF16),
+            jax.ShapeDtypeStruct((n_tok, rank, width), BF16),
         ),
         in_specs=[vmem] * 4,
         out_specs=(vmem,) * 4,
@@ -353,13 +384,11 @@
             pltpu.VMEM((n_tok - 1, rows, cols), BF16),
             pltpu.VMEM((n_tok - 1, rows, cols), BF16),
             pltpu.VMEM((n_tok, count, cols), BF16),
-            pltpu.VMEM((n_tok, width, rank), BF16),
-            pltpu.VMEM((n_tok, rank, width), BF16),
             sems((2, n_tok + 1, n_chip)),
             sems((2, n_tok + 1, n_chip - 1)),
             sems((2, n_tok - 1)),
             sems((2, n_tok - 1)),
-            sems((2, n_tok - 1, 2)),
+            sems((2, 2, n_tok - 1, 2)),
         ],
         compiler_params=pltpu.CompilerParams(
             collective_id=1, has_side_effects=True, vmem_limit_bytes=56 * 1024 * 1024
@@ -407,6 +436,8 @@
     input_gradient, total, grad_out_a, grad_in_b = reduce_outputs(
         dense, terms, oa.astype(BF16), ib.astype(BF16)
     )
+    grad_out_a = grad_out_a.reshape(-1, rank).astype(F32)
+    grad_in_b = grad_in_b.transpose(1, 0, 2).reshape(rank, -1).astype(F32)
     return (input_gradient, total[rank:].T, grad_in_b, grad_out_a, total[:rank])
 
 

time: 170 us -> 170 us (level)
  local copies, waits for them, and re-layouts: 8.51 us -> 4.71 us
  other arithmetic: 5.68 us -> 7.92 us
  Pallas kernels: 124 us -> 126 us
    unnamed x14 -> x17, local copies, waits for them, and re-layouts: 7 us -> 2.8 us
    pallas_call x1, Pallas kernels: 56.2 us -> 58.5 us  [reduce_outputs(): pl.pallas_call(functools.partial(reduce_kernel, n_tok, n_hid), out_shape=...]
    convert_element_type x0 -> x2, other arithmetic: none -> 2.23 us  [the longest x1 1.16 us: local(): grad_in_b = grad_in_b.transpose(1, 0, 2).reshape(rank, -1).astype(F32)]
where the time goes in v4:
time: 170 us
  Pallas kernels  126 us (74%)
  matrix products  30.4 us (18%)
  other arithmetic  7.92 us (5%)
  local copies, waits for them, and re-layouts  4.71 us (3%)
    pallas_call x1, Pallas kernels, gather_inputs(): pl.pallas_call(functools.partial(gather_kernel, n_tok, n_hid), out_shape=...  67.5 us
    pallas_call x1, Pallas kernels, reduce_outputs(): pl.pallas_call(functools.partial(reduce_kernel, n_tok, n_hid), out_shape=...  58.5 us
    dot_general x14, matrix products, dot(): lax.dot_general(left, right, (dims, ((), ())), preferred_element_type=F32)  30.4 us

profile of v4, /device:TPU:0, one launch (start us, length us, event | category | flops | bytes accessed | tf_op | source)
XLA Modules:
  0.0 170.0 jit_solution(14878840731036724119)
XLA Ops:
  0.6 0.0 copy-start
  0.7 1.0 dynamic-slice_multiply_fusion
  1.6 0.9 dynamic-slice_multiply_fusion.1
  2.6 67.5 %shard_map.119 = (bf16[2048,1024]{1,0:T(8,128)(2,1)}, bf16[2048,1024]{1,0:T(8,128)(2,1)}, bf16[1024,512]{1,0:T(8,128)(2,1)}, bf16[512,1024]{1,0:T(8,128)(2,1)}, bf16[1024,128]{1,0:T(8,128)(2,1)}) custom-call(bf16[512,128]{1,0:T(8,128)(2,1)} %tokens.1, bf16[512,128]{1,0:T(8,128)(2,1)} %cotangent.1, bf16[256,2048]{1,0:T(8,128)(2,1)} %w_in.1, ...), custom_call_target="tpu_custom_call" | custom-call | tf_op jit(solution)/shard_map/pallas_call | solution.py:170
  70.1 0.0 copy-start.4
  70.1 1.1 broadcast_multiply_fusion
  71.2 3.9 %reduce-precision_convert_fusion.2 = (bf16[2048,128]{0,1:T(8,128)(2,1)S(1)}, bf16[2048,128]{0,1:T(8,128)(2,1)S(1)}) fusion(bf16[2048,1024]{1,0:T(8,128)(2,1)} %get-tuple-element.16, bf16[1024,128]{1,0:T(8,128)(2,1)} %get-tuple-element.18), kind=kOutput, calls=%fused_computation.17 | convolution fusion | flops 537919488 | bytes 5505024 | tf_op jit(solution)/shard_map/dot_general | solution.py:35
  75.2 0.0 copy-start.6
  75.2 0.0 copy-done
  75.2 0.0 copy-done.4
  75.2 1.5 reduce-precision_convert_fusion.3
  76.7 0.0 copy-done.6
  76.8 0.0 copy-start.1
  76.8 0.0 copy-start.5
  76.8 2.4 %fusion.45 = f32[2048,512]{1,0:T(8,128)S(1)} fusion(bf16[2048,1024]{1,0:T(8,128)(2,1)S(1)} %copy-done.4, bf16[512,1024]{1,0:T(8,128)(2,1)S(1)} %copy-done.6), kind=kOutput, calls=%fused_computation.72 | convolution fusion | flops 2147483648 | bytes 9437184 | tf_op jit(solution)/shard_map/dot_general | solution.py:35
  79.2 0.0 copy-done.1
  79.2 0.0 copy-done.5
  79.2 2.4 %fusion.46 = f32[2048,512]{1,0:T(8,128)S(1)} fusion(bf16[2048,1024]{1,0:T(8,128)(2,1)S(1)} %copy-done.1, bf16[1024,512]{1,0:T(8,128)(2,1)S(1)} %copy-done.5), kind=kOutput, calls=%fused_computation.73 | convolution fusion | flops 2147483648 | bytes 9437184 | tf_op jit(solution)/shard_map/dot_general | solution.py:35
  81.6 0.8 convolution_add_fusion.1
  82.4 3.4 %fusion.6 = bf16[2048,512]{1,0:T(8,128)(2,1)S(1)} fusion(f32[2048,512]{1,0:T(8,128)S(1)} %convolution_add_fusion.1, f32[2048,512]{1,0:T(8,128)S(1)} %fusion.45, bf16[2048,128]{0,1:T(8,128)(2,1)S(1)} %get-tuple-element.38, bf16[2048,128]{0,1:T(8,128)(2,1)S(1)} %get-tuple-element.37, bf16[512,128]{1,0:T(8,128)(2,1)S(1)} %dynamic-slice_multiply_fusion.1), kind=kOutput, calls=%fused_computation.9 | convolution fusion | flops 560463872 | bytes 11665408 | tf_op jit(solution)/shard_map/dot_general | solution.py:35
  85.8 1.5 fusion.17
  87.4 2.6 %reduce-precision_convert_fusion = (bf16[2048,128]{0,1:T(8,128)(2,1)S(1)}, bf16[2048,128]{0,1:T(8,128)(2,1)S(1)}) fusion(bf16[2048,128]{1,0:T(8,128)(2,1)} %param.14, s32[]{:T(128)S(6)} %select_n.4, f32[2048,512]{1,0:T(8,128)S(1)} %convolution_add_fusion.1), kind=kOutput, calls=%fused_computation.13 | convolution fusion | flops 278921216 | bytes 5373956 | tf_op jit(solution)/shard_map/dot_general | solution.py:35
  89.9 0.7 fusion.16
  90.6 0.7 fusion.22.ib
  91.3 0.7 fusion.24.oa
  92.0 1.3 fusion.11
  93.3 1.7 %reduce-precision_convert_fusion.1 = (bf16[2048,128]{0,1:T(8,128)(2,1)S(1)}, bf16[2048,128]{0,1:T(8,128)(2,1)S(1)}) fusion(bf16[2048,512]{1,0:T(8,128)(2,1)S(1)} %fusion.6, bf16[128,2048]{1,0:T(8,128)(2,1)} %param.13, s32[]{:T(128)S(6)} %select_n.4), kind=kOutput, calls=%fused_computation.15 | convolution fusion | flops 269484032 | bytes 3276804 | tf_op jit(solution)/shard_map/dot_general | solution.py:35
  95.1 1.3 fusion.15
  96.3 0.2 slice_add_fusion
  96.5 1.1 maximum_multiply_fusion.terms
  97.6 2.4 %fusion.47 = f32[2048,1024]{1,0:T(8,128)S(1)} fusion(bf16[2048,512]{1,0:T(8,128)(2,1)S(1)} %fusion.6, bf16[1024,512]{1,0:T(8,128)(2,1)S(1)} %copy-done.5), kind=kOutput, calls=%fused_computation.74 | convolution fusion | flops 2147483648 | bytes 11534336 | tf_op jit(solution)/shard_map/dot_general | solution.py:35
  100.0 4.6 %convolution_add_fusion.dense = f32[2048,1024]{1,0:T(8,128)} fusion(f32[2048,1024]{1,0:T(8,128)S(1)} %fusion.47, bf16[2048,128]{0,1:T(8,128)(2,1)S(1)} %get-tuple-element.36, bf16[2048,128]{0,1:T(8,128)(2,1)S(1)} %get-tuple-element.35, bf16[1024,128]{1,0:T(8,128)(2,1)S(1)} %broadcast_multiply_fusion), kind=kOutput, calls=%fused_computation.2 | convolution fusion | flops 1078984704 | bytes 18087936 | tf_op jit(solution)/shard_map/dot_general | solution.py:35
  104.5 58.5 %shard_map.120 = (f32[512,128]{1,0:T(8,128)}, f32[256,128]{1,0:T(8,128)}, bf16[4,512,128]{2,1,0:T(8,128)(2,1)}, bf16[4,128,512]{2,1,0:T(8,128)(2,1)}) custom-call(f32[2048,1024]{1,0:T(8,128)} %convolution_add_fusion.dense, f32[256,1024]{1,0:T(8,128)} %maximum_multiply_fusion.terms, bf16[512,128]{1,0:T(8,128)(2,1)} %fusion.24.oa, bf16[128,512]{1,0:T(8,128)(2,1)} %fusion.22.ib), custom_call_target="tpu_custom_call" | custom-call | tf_op jit(solution)/shard_map/pallas_call | solution.py:365
  163.0 0.0 copy-start.2
  163.0 0.0 copy-start.3
  163.1 1.6 fusion.44
  164.6 0.7 copy.15
  165.4 1.2 convert_bitcast_fusion
  166.5 0.3 copy.14
  166.9 1.3 copy.16
  168.2 0.0 copy-done.2
  168.2 1.1 bitcast_convert_fusion
  169.3 0.0 copy-done.3
  169.3 0.7 copy.18
Async XLA Ops:
  0.6 74.6 %copy-start = (bf16[128,1024]{1,0:T(8,128)(2,1)S(1)}, bf16[128,1024]{1,0:T(8,128)(2,1)}, u32[]{:S(2)}) copy-start(bf16[128,1024]{1,0:T(8,128)(2,1)} %param.15) | copy-start | bytes 786436
  70.1 5.1 %copy-start.4 = (bf16[2048,1024]{1,0:T(8,128)(2,1)S(1)}, bf16[2048,1024]{1,0:T(8,128)(2,1)}, u32[]{:S(2)}) copy-start(bf16[2048,1024]{1,0:T(8,128)(2,1)} %get-tuple-element.14) | copy-start | bytes 12582916
  75.2 1.6 copy-start.6
  76.8 2.5 %copy-start.1 = (bf16[2048,1024]{1,0:T(8,128)(2,1)S(1)}, bf16[2048,1024]{1,0:T(8,128)(2,1)}, u32[]{:S(2)}) copy-start(bf16[2048,1024]{1,0:T(8,128)(2,1)} %get-tuple-element.16) | copy-start | bytes 12582916
  76.8 2.5 %copy-start.5 = (bf16[1024,512]{1,0:T(8,128)(2,1)S(1)}, bf16[1024,512]{1,0:T(8,128)(2,1)}, u32[]{:S(2)}) copy-start(bf16[1024,512]{1,0:T(8,128)(2,1)} %get-tuple-element.17) | copy-start | bytes 3145732
  163.0 5.2 %copy-start.2 = (bf16[4,512,128]{2,1,0:T(8,128)(2,1)S(1)}, bf16[4,512,128]{2,1,0:T(8,128)(2,1)}, u32[]{:S(2)}) copy-start(bf16[4,512,128]{2,1,0:T(8,128)(2,1)} %get-tuple-element.22) | copy-start | bytes 1572868
  163.0 6.2 %copy-start.3 = (f32[512,128]{1,0:T(8,128)S(1)}, f32[512,128]{1,0:T(8,128)}, u32[]{:S(2)}) copy-start(f32[512,128]{1,0:T(8,128)} %get-tuple-element.50) | copy-start | bytes 786436
